TPU v7x, 1024 devices: a whole 4x4x32 slice. The times are simulated.
1024 devices in a mesh: ep: 32 (over y, x, core), tp: 32 (over z).
Axes of the slice: x: 4, y: 4, z: 32, core: 2. Of those that a mesh axis runs over, the one named last changes fastest.
Arguments:
- attn: bfloat16 [2048, 4096], P('ep', 'tp'), may hold values from -6 to 6
- norm_gain: float32 [4096], replicated, may hold values from 0.5 to 1.5
- w_gate: bfloat16 [32, 1792, 4096], P('ep', 'tp'), may hold values from -0.09375 to 0.09375
- w_up: bfloat16 [32, 1792, 4096], P('ep', 'tp'), may hold values from -0.09375 to 0.09375
- w_down: bfloat16 [32, 1792, 4096], P('ep', 'tp'), may hold values from -0.0625 to 0.0625
- expert_ids: int32 [2048, 2], P('ep'), may hold values from 0 to 7, all different within a row; in each aligned block of 64 rows (0 to 63, 64 to 127, ...) at most 24 rows name the same one
- gate_fix: int32 [2048, 2], P('ep'), may hold values from 1 to 65535, as said below
Outputs:
- moe_out: bfloat16 [2048, 4096], P('ep', 'tp')
Inputs may be any that keep to these rules, and one draw needn't show every extreme that they name: `expert_ids`: among the tokens of one ep index (64 rows), no expert is named by more than 24 routes, a bound that some block reaches; a row names 2 different experts. `gate_fix`: the 2 entries of a row sum to 65536.
All inputs are finite; a program needn't handle non-finite values.
Results may differ from a plain program's by a relative error of at most 0.0065.
Values may be sent and summed in bfloat16 or wider, within the bound.
No kernel may reach another device: no remote copies, remote signals or barrier semaphores. Data moves between devices by JAX's collectives and lax.ppermute only.
A program may use at most 32 MiB of HBM per device.

v0:
```python
import jax
import jax.numpy as jnp
from jax import lax
from jax.sharding import PartitionSpec as P

EXPERTS = 8


def route_ordinal(route_ids):
    flat_ids = route_ids.reshape(-1)
    onehot = (flat_ids[:, None] == jnp.arange(EXPERTS, dtype=jnp.int32)[None, :]).astype(jnp.int32)
    before = jnp.cumsum(onehot, axis=0) - onehot
    return jnp.sum(before * onehot, axis=1)


def contract_last(left, right):
    return lax.dot_general(
        left, right, (((1,), (1,)), ((), ())), preferred_element_type=jnp.float32
    )


def body(attn, norm_gain, w_gate, w_up, w_down, expert_ids, gate_fix):
    owners_count = lax.axis_size("ep")
    row_tok, feature_cols = attn.shape
    model_width = norm_gain.shape[0]
    top_count = expert_ids.shape[1]
    slot_cap = 3 * row_tok // 8
    slices = owners_count // EXPERTS
    key_count = EXPERTS * slot_cap
    ordinal = route_ordinal(expert_ids)
    target = expert_ids.reshape(-1) * slot_cap + ordinal
    hits = (target[:, None] == jnp.arange(key_count, dtype=jnp.int32)[None, :]).astype(jnp.float32)
    hits_split = hits.reshape(row_tok, top_count, key_count)
    pick_rows = jnp.sum(hits_split, axis=1).T.astype(jnp.bfloat16)
    route_weight = gate_fix.astype(jnp.float32) / 65536.0
    combine_map = jnp.sum(hits_split * route_weight[:, :, None], axis=1)
    full_rows = lax.all_gather(attn, "tp", axis=1, tiled=True)
    values = full_rows.astype(jnp.float32)
    inverse_rms = lax.rsqrt(jnp.mean(values * values, axis=-1, keepdims=True) + 1e-05)
    normed = (values * inverse_rms * norm_gain).astype(jnp.bfloat16)
    by_expert = jnp.dot(pick_rows, normed, preferred_element_type=jnp.float32).astype(jnp.bfloat16)
    by_expert = by_expert.reshape(EXPERTS, slot_cap, normed.shape[1])
    outgoing = jnp.repeat(by_expert, slices, axis=0)
    incoming = lax.all_to_all(outgoing, "ep", split_axis=0, concat_axis=0, tiled=True)
    slot_rows = incoming.reshape(owners_count * slot_cap, model_width)
    gate_act = contract_last(slot_rows, w_gate[0])
    up_act = contract_last(slot_rows, w_up[0])
    hidden_act = (jax.nn.silu(gate_act) * up_act).astype(jnp.bfloat16)
    slice_out = jnp.dot(hidden_act, w_down[0], preferred_element_type=jnp.float32)
    slice_out = slice_out.reshape(owners_count, slot_cap, model_width)
    shares = lax.psum_scatter(slice_out, "tp", scatter_dimension=2, tiled=True)
    returned = lax.all_to_all(shares, "ep", split_axis=0, concat_axis=0, tiled=True)
    expert_sums = jnp.sum(returned.reshape(EXPERTS, slices, slot_cap, shares.shape[2]), axis=1)
    combined = jnp.dot(
        combine_map,
        expert_sums.reshape(key_count, shares.shape[2]),
        precision=lax.Precision.HIGHEST,
        preferred_element_type=jnp.float32,
    )
    return combined.astype(jnp.bfloat16)


def solution(mesh):
    in_specs = (
        P("ep", "tp"),
        P(),
        P("ep", "tp", None),
        P("ep", "tp", None),
        P("ep", "tp", None),
        P("ep", None),
        P("ep", None),
    )
    out_specs = P("ep", "tp")
    return jax.shard_map(body, mesh=mesh, in_specs=in_specs, out_specs=out_specs, check_vma=False)
```

profile of v0, /device:TPU:1, one launch (start us, length us, event | category | flops | bytes accessed | tf_op | source)
XLA Modules:
  0.0 360.8 jit_solution(15468347831729256797)
XLA Ops:
  6.5 0.0 copy-start
  6.5 0.0 reduce-scatter.2.cloned.1.call-start
  6.5 0.7 convert_multiply_fusion.2
  7.3 0.8 copy.23
  8.0 0.1 eq.29
  8.2 0.1 fusion.12
  8.3 0.2 reduce_window_sum.11
  8.5 0.2 select_reduce_fusion.1
  8.6 0.1 reduce_sum.48
  8.8 0.1 copy.24
  8.8 0.7 multiply_add_fusion
  9.5 58.1 %all_gather.3 = bf16[64,4096]{1,0:T(8,128)(2,1)S(1)} all-gather(bf16[64,128]{1,0:T(8,128)(2,1)} %param.7), channel_id=1, replica_groups=mesh['ep'=32,'tp'=32] {'tp'}, dimensions={1}, use_global_device_ids=true | all-gather | bytes 540672 | tf_op jit(solution)/shard_map/all_gather | solution.py:37
  67.6 0.2 fusion.1
  67.9 0.1 convert_reduce_fusion
  68.0 1.3 convolution_convert_fusion
  69.3 0.8 broadcast_in_dim.2
  70.1 0.0 copy-start.2
  70.1 94.6 %all_to_all.10 = bf16[32,24,4096]{2,1,0:T(8,128)(2,1)S(1)} all-to-all(bf16[32,24,4096]{2,1,0:T(8,128)(2,1)S(1)} %bitcast.25), channel_id=1, replica_groups=mesh['ep'=32,'tp'=32] {'ep'}, dimensions={0} | all-to-all | bytes 12582912 | tf_op jit(solution)/shard_map/all_to_all | solution.py:44
  164.7 0.0 copy-start.1
  164.7 0.0 copy-done.2
  164.7 2.0 fusion.10
  166.8 0.0 copy-done.1
  166.8 2.0 fusion
  168.8 0.2 copy.25
  169.0 0.0 copy-done
  169.0 6.4 %fusion.7 = f32[32,24,4096]{2,1,0:T(8,128)} fusion(bf16[32,24,56]{2,1,0:T(8,128)(2,1)S(1)} %bitcast.27, bf16[1,56,4096]{2,1,0:T(8,128)(2,1)S(1)} %copy-done), kind=kOutput, calls=%fused_computation.11 | convolution fusion | flops 352321536 | bytes 13127680 | tf_op jit(solution)/shard_map/dot_general | solution.py:49
  175.4 0.0 reduce-scatter.2.cloned.1.call-update
  175.4 144.6 %reduce-scatter.2.cloned.1.call-done = f32[32,24,128]{2,1,0:T(8,128)} async-done(((f32[32,24,4096]{2,1,0:T(8,128)}), f32[32,24,128]{2,1,0:T(8,128)}) %reduce-scatter.2.cloned.1.call-update) | async-done | bytes 393232 | tf_op jit(solution)/shard_map/reduce_scatter | solution.py:51
  320.0 33.1 %all_to_all.11 = f32[32,24,128]{2,1,0:T(8,128)S(1)} all-to-all(f32[32,24,128]{2,1,0:T(8,128)} %reduce-scatter.2.cloned.1.call-done), channel_id=1, replica_groups=mesh['ep'=32,'tp'=32] {'ep'}, dimensions={0} | all-to-all | bytes 786432 | tf_op jit(solution)/shard_map/all_to_all | solution.py:52
  353.2 0.8 convolution_convert_fusion.1
  (2 shorter events, 0.0 us)
Async XLA Ops:
  6.5 162.4 %copy-start = (bf16[1,56,4096]{2,1,0:T(8,128)(2,1)S(1)}, bf16[1,56,4096]{2,1,0:T(8,128)(2,1)}, u32[]{:S(2)}) copy-start(bf16[1,56,4096]{2,1,0:T(8,128)(2,1)} %param.11) | copy-start | bytes 1376260
  6.5 313.5 %reduce-scatter.2.cloned.1.call-start = ((), (), s32[]{:S(2)}) async-start(), calls=%async_computation.3 | async-start | bytes 12976128 | tf_op jit(solution)/shard_map/reduce_scatter | solution.py:51
  70.1 94.6 %copy-start.2 = (bf16[1,56,4096]{2,1,0:T(8,128)(2,1)S(1)}, bf16[1,56,4096]{2,1,0:T(8,128)(2,1)}, u32[]{:S(2)}) copy-start(bf16[1,56,4096]{2,1,0:T(8,128)(2,1)} %param.9) | copy-start | bytes 1376260
  164.7 2.0 copy-start.1
Sparse Core Ops, SparseCore 0:
  175.5 144.4 reduce-scatter.1
where the time goes:
time: 361 us
  blocking collectives  186 us (52%)
  waiting for transfers between devices  145 us (40%)
  between operations  13.5 us (4%)
  matrix products  12.6 us (3%)
    reduce_scatter x1, waiting for transfers between devices, body(): shares = lax.psum_scatter(slice_out, 'tp', scatter_dimension=2, tiled=True)  145 us
    all_to_all x1, blocking collectives, body(): lax.all_to_all(outgoing, 'ep', split_axis=0, concat_axis=0, tiled=True)  94.6 us
    all_gather x1, blocking collectives, body(): full_rows = lax.all_gather(attn, 'tp', axis=1, tiled=True)  58.1 us
    all_to_all x1, blocking collectives, body(): lax.all_to_all(shares, 'ep', split_axis=0, concat_axis=0, tiled=True)  33.1 us
  transfers between devices with their start and end apart: 1, of which 1 were waited for; matrix products, arithmetic and copies ran while one was open for 0% of the time, Pallas kernels for 0%

commit v1 on v0

v1 whole, which is shorter than its diff:
```python
import jax
import jax.numpy as jnp
from jax import lax
from jax.sharding import Mesh
from jax.sharding import PartitionSpec as P

EXPERTS = 8
EP = ("eh", "xl", "core")
TP = ("zh", "zl")
QUAD = ("xl", "core")
SWAP = [(0, 1), (1, 0)]


def route_ordinal(route_ids):
    flat_ids = route_ids.reshape(-1)
    onehot = (flat_ids[:, None] == jnp.arange(EXPERTS, dtype=jnp.int32)[None, :]).astype(jnp.float32)
    count = flat_ids.shape[0]
    earlier = (jnp.arange(count)[:, None] > jnp.arange(count)[None, :]).astype(jnp.float32)
    before = jnp.dot(earlier, onehot, preferred_element_type=jnp.float32)
    return jnp.sum(before * onehot, axis=1).astype(jnp.int32)


def contract_last(left, right):
    return lax.dot_general(
        left, right, (((1,), (1,)), ((), ())), preferred_element_type=jnp.float32
    )


def pair_up(mine, other, position):
    low = jnp.where(position == 0, mine, other)
    high = jnp.where(position == 0, other, mine)
    return jnp.stack([low, high])


def body(attn, norm_gain, w_gate, w_up, w_down, expert_ids, gate_fix):
    owners = lax.axis_size(EP)
    n_zh, n_zl = lax.axis_size("zh"), lax.axis_size("zl")
    xl, core = lax.axis_index("xl"), lax.axis_index("core")
    row_tok, cols = attn.shape
    width = norm_gain.shape[0]
    top_count = expert_ids.shape[1]
    cap = 3 * row_tok // 8
    slices = owners // EXPERTS
    part = width // slices
    key_count = EXPERTS * cap
    hid = w_gate.shape[1]

    stacked = jnp.concatenate([w_gate, w_up, w_down], axis=0)
    half = width // 2
    keep_x = lax.dynamic_slice_in_dim(stacked, xl * half, half, axis=2)
    send_x = lax.dynamic_slice_in_dim(stacked, (1 - xl) * half, half, axis=2)
    got_x = lax.ppermute(send_x, "xl", SWAP)

    rows = lax.all_gather(attn, "zl", axis=1, tiled=True)
    rows = lax.all_gather(rows, "zh", axis=1, tiled=True)
    rows, got_x = lax.optimization_barrier((rows, got_x))

    pair_x = pair_up(keep_x, got_x, xl)
    keep_c = lax.dynamic_slice_in_dim(pair_x, core * part, part, axis=3)
    send_c = lax.dynamic_slice_in_dim(pair_x, (1 - core) * part, part, axis=3)
    got_c = lax.ppermute(send_c, "core", SWAP)

    ordinal = route_ordinal(expert_ids)
    target = expert_ids.reshape(-1) * cap + ordinal
    hits = (target[:, None] == jnp.arange(key_count, dtype=jnp.int32)[None, :]).astype(jnp.float32)
    hits = hits.reshape(row_tok, top_count, key_count)
    pick_rows = jnp.sum(hits, axis=1).T.astype(jnp.bfloat16)
    high = (gate_fix // 256).astype(jnp.float32)
    low = (gate_fix % 256).astype(jnp.float32)
    combine_map = jnp.concatenate(
        [jnp.sum(hits * high[:, :, None], axis=1), jnp.sum(hits * low[:, :, None], axis=1)], axis=0
    ).astype(jnp.bfloat16)

    values = rows.astype(jnp.float32)
    inverse_rms = lax.rsqrt(jnp.mean(values * values, axis=-1, keepdims=True) + 1e-05)
    normed = (values * inverse_rms * norm_gain).astype(jnp.bfloat16)
    by_expert = jnp.dot(pick_rows, normed, preferred_element_type=jnp.float32).astype(jnp.bfloat16)
    outgoing = by_expert.reshape(EXPERTS, cap, slices, part).transpose(0, 2, 1, 3)
    incoming = lax.all_to_all(outgoing.reshape(owners, cap, part), EP, split_axis=0, concat_axis=0, tiled=True)
    incoming, got_c = lax.optimization_barrier((incoming, got_c))
    slot_rows = incoming.reshape(owners * cap, part)

    quad = pair_up(keep_c, got_c, core).transpose(2, 1, 0, 3, 4)
    hidden_quad = slices * hid
    quad = quad.reshape(3, hidden_quad, part)
    gate_part = contract_last(slot_rows, quad[0]).astype(jnp.bfloat16)
    up_part = contract_last(slot_rows, quad[1]).astype(jnp.bfloat16)
    group = owners * cap // slices
    parts = jnp.stack(
        [gate_part.reshape(slices, group, hidden_quad), up_part.reshape(slices, group, hidden_quad)], axis=1
    )
    parts = lax.all_to_all(parts, QUAD, split_axis=0, concat_axis=0, tiled=True)
    sums = jnp.sum(parts.astype(jnp.float32), axis=0)
    hidden_act = (jax.nn.silu(sums[0]) * sums[1]).astype(jnp.bfloat16)
    spread = jnp.broadcast_to(hidden_act[None], (slices,) + hidden_act.shape)
    hidden_all = lax.all_to_all(spread, QUAD, split_axis=0, concat_axis=0, tiled=True)
    slice_out = jnp.dot(hidden_all.reshape(owners * cap, hidden_quad), quad[2], preferred_element_type=jnp.float32)
    slice_out = slice_out.astype(jnp.bfloat16).reshape(owners, cap, part)
    returned = lax.all_to_all(slice_out, EP, split_axis=0, concat_axis=0, tiled=True)

    returned = returned.reshape(EXPERTS, slices, cap, part).transpose(0, 2, 1, 3).reshape(key_count, width)
    both = jnp.dot(combine_map, returned, preferred_element_type=jnp.float32)
    combined = both[:row_tok] * (1.0 / 256.0) + both[row_tok:] * (1.0 / 65536.0)
    pieces = combined.astype(jnp.bfloat16).reshape(row_tok, n_zh, n_zl, cols).transpose(2, 1, 0, 3)
    pieces = lax.all_to_all(pieces, "zl", split_axis=0, concat_axis=0, tiled=True)
    pieces = jnp.sum(pieces.astype(jnp.float32), axis=0).astype(jnp.bfloat16)
    pieces = lax.all_to_all(pieces, "zh", split_axis=0, concat_axis=0, tiled=True)
    return jnp.sum(pieces.astype(jnp.float32), axis=0).astype(jnp.bfloat16)


def solution(mesh):
    n_ep, n_tp = mesh.devices.shape
    near = 4 if n_tp % 4 == 0 else 1
    fine = Mesh(
        mesh.devices.reshape(n_ep // 4, 2, 2, n_tp // near, near), ("eh", "xl", "core", "zh", "zl")
    )
    in_specs = (
        P(EP, TP),
        P(),
        P(EP, TP, None),
        P(EP, TP, None),
        P(EP, TP, None),
        P(EP, None),
        P(EP, None),
    )
    return jax.shard_map(body, mesh=fine, in_specs=in_specs, out_specs=P(EP, TP), check_vma=False)
```

time: 361 us -> 228 us (0.63)
  the two profiles are of different devices: /device:TPU:1 before, /device:TPU:2 now
where the time goes in v1:
time: 228 us
  blocking collectives  165 us (72%)
  starting transfers between devices  25.7 us (11%)
  waiting for transfers between devices  19.5 us (9%)
  local copies, waits for them, and re-layouts  9.06 us (4%)
  matrix products  5.91 us (3%)
  other arithmetic  2.42 us (1%)
    all_gather x1, blocking collectives, body(): rows = lax.all_gather(rows, 'zh', axis=1, tiled=True)  43.3 us
    all_to_all x1, blocking collectives, body(): lax.all_to_all(pieces, 'zh', split_axis=0, concat_axis=0, tiled=True)  41.1 us
    all_to_all x1, blocking collectives, body(): lax.all_to_all(slice_out, EP, split_axis=0, concat_axis=0, tiled=True)  26 us
    all_to_all x1, blocking collectives, body(): lax.all_to_all(pieces, 'zl', split_axis=0, concat_axis=0, tiled=True)  17.8 us
    all_to_all x1, waiting for transfers between devices, body(): lax.all_to_all(outgoing.reshape(owners, cap, part), EP, split_axis=0, con...  17.5 us
    ppermute x1, starting transfers between devices, body(): got_x = lax.ppermute(send_x, 'xl', SWAP)  15.1 us
    all_to_all x1, blocking collectives, body(): parts = lax.all_to_all(parts, QUAD, split_axis=0, concat_axis=0, tiled=True)  14.6 us
    all_gather x1, blocking collectives, body(): rows = lax.all_gather(attn, 'zl', axis=1, tiled=True)  12 us
  transfers between devices with their start and end apart: 3, of which 2 were waited for; matrix products, arithmetic and copies ran while one was open for 1% of the time, Pallas kernels for 0%

profile of v1, /device:TPU:2, one launch (start us, length us, event | category | flops | bytes accessed | tf_op | source)
XLA Modules:
  0.0 227.6 jit_solution(15755970561226641032)
XLA Ops:
  0.0 1.1 constant_dynamic-update-slice_fusion.2
  1.1 1.1 constant_dynamic-update-slice_fusion.1
  2.3 0.1 constant_dynamic-slice_fusion
  2.3 15.1 %collective-permute-start = (bf16[3,56,2048]{2,1,0:T(8,128)(2,1)S(1)}, bf16[3,56,2048]{2,1,0:T(8,128)(2,1)S(1)}, u32[]{:S(2)}, u32[]{:S(2)}) collective-permute-start(bf16[3,56,2048]{2,1,0:T(8,128)(2,1)S(1)} %constant_dynamic-slice_fusion), channel_id=1, source_target_pairs={{0,64},{64,0},{1,65},{65,1},{2,66},{66,2},{3,67},{67,3},{4,68},{68... | collective-permute-start | bytes 2064392 | tf_op jit(solution)/shard_map/ppermute | solution.py:52
  17.4 0.1 copy.77
  17.5 0.1 eq.39
  17.7 0.1 fusion
  17.8 0.1 convert_element_type.60
  18.0 0.1 copy.78
  18.1 12.0 %all_gather.6 = bf16[64,512]{1,0:T(8,128)(2,1)S(1)} all-gather(bf16[64,128]{1,0:T(8,128)(2,1)S(1)} %copy-done.6), channel_id=1, replica_groups=mesh['eh'=8,'xl'=2,'core'=2,'zh'=8,'zl'=4] {'zl'}, dimensions={1}, use_global_device_ids=true | all-gather | bytes 81920 | tf_op jit(solution)/shard_map/all_gather | solution.py:54
  30.1 0.1 select_reduce_fusion.1
  30.2 43.3 %all_gather.7 = bf16[64,4096]{1,0:T(8,128)(2,1)S(1)} all-gather(bf16[64,512]{1,0:T(8,128)(2,1)S(1)} %all_gather.6), channel_id=1, replica_groups=mesh['eh'=8,'xl'=2,'core'=2,'zh'=8,'zl'=4] {'zh'}, dimensions={1}, use_global_device_ids=true | all-gather | bytes 589824 | tf_op jit(solution)/shard_map/all_gather | solution.py:55
  73.6 0.2 fusion.1
  73.8 0.6 copy-done.2
  74.4 0.6 convolution_convert_fusion
  75.0 1.2 reshape.63
  76.2 1.6 copy.79
  77.9 8.6 %all-to-all-start = ((bf16[32,24,1024]{2,1,0:T(8,128)(2,1)}), bf16[32,24,1024]{2,1,0:T(8,128)(2,1)}, u32[]{:S(2)}, u32[]{:S(2)}) async-start(bf16[32,24,1024]{2,1,0:T(8,128)(2,1)} %bitcast.1), calls=%async_computation | async-start | bytes 3145728 | tf_op jit(solution)/shard_map/all_to_all | solution.py:79
  86.6 0.3 select_bitcast_fusion.2
  86.9 0.1 fusion.7
  87.0 2.0 collective-permute-start.1
  89.0 2.0 collective-permute-done.1
  91.0 17.5 %all-to-all-done = bf16[32,24,1024]{2,1,0:T(8,128)(2,1)} async-done(((bf16[32,24,1024]{2,1,0:T(8,128)(2,1)}), bf16[32,24,1024]{2,1,0:T(8,128)(2,1)}, u32[]{:S(2)}, u32[]{:S(2)}) %all-to-all-start) | async-done | bytes 1572896 | tf_op jit(solution)/shard_map/all_to_all | solution.py:79
  108.5 0.3 select_bitcast_fusion.1
  108.9 0.1 maximum_bitcast_fusion
  109.0 0.1 fusion.22
  109.2 2.1 convolution_convert_fusion.3
  111.2 0.2 copy.82
  111.4 2.1 convolution_convert_fusion.2
  113.5 0.2 copy.83
  113.7 0.2 pad_maximum_fusion
  113.8 0.1 copy.84
  113.9 14.6 %all_to_all.30 = bf16[4,2,192,224]{3,2,1,0:T(8,128)(2,1)S(1)} all-to-all(bf16[4,2,192,224]{3,2,1,0:T(8,128)(2,1)S(1)} %copy.84), channel_id=1, replica_groups=mesh['eh'=8,'xl'=2,'core'=2,'zh'=8,'zl'=4] {'xl','core'}, dimensions={0} | all-to-all | bytes 1376256 | tf_op jit(solution)/shard_map/all_to_all | solution.py:92
  128.5 0.1 convert_reduce_fusion
  128.6 0.1 fusion.12
  128.7 9.8 %all_to_all.31 = bf16[4,192,224]{2,1,0:T(8,128)(2,1)S(1)} all-to-all(bf16[4,192,224]{2,1,0:T(8,128)(2,1)S(1)} %broadcast_in_dim.5), channel_id=1, replica_groups=mesh['eh'=8,'xl'=2,'core'=2,'zh'=8,'zl'=4] {'xl','core'}, dimensions={0} | all-to-all | bytes 688128 | tf_op jit(solution)/shard_map/all_to_all | solution.py:96
  138.5 0.6 convolution_convert_fusion.1
  139.1 26.0 %all_to_all.32 = bf16[32,24,1024]{2,1,0:T(8,128)(2,1)S(1)} all-to-all(bf16[32,24,1024]{2,1,0:T(8,128)(2,1)S(1)} %bitcast.45), channel_id=1, replica_groups=mesh['eh'=8,'xl'=2,'core'=2,'zh'=8,'zl'=4] {'eh','xl','core'}, dimensions={0} | all-to-all | bytes 3145728 | tf_op jit(solution)/shard_map/all_to_all | solution.py:99
  165.1 1.2 copy.85
  166.3 0.6 copy.90
  167.0 0.4 fusion.13
  167.4 0.1 fusion.5
  167.5 0.4 reshape.70
  167.9 0.1 copy.92
  168.0 17.8 %all_to_all.33 = bf16[4,8,64,128]{3,1,2,0:T(8,128)(2,1)S(1)} all-to-all(bf16[4,8,64,128]{3,1,2,0:T(8,128)(2,1)S(1)} %bitcast.48), channel_id=1, replica_groups=mesh['eh'=8,'xl'=2,'core'=2,'zh'=8,'zl'=4] {'zl'}, dimensions={0} | all-to-all | bytes 1048576 | tf_op jit(solution)/shard_map/all_to_all | solution.py:105
  185.8 0.1 reduce_sum.84
  185.9 41.1 %all_to_all.34 = bf16[8,64,128]{2,1,0:T(8,128)(2,1)S(1)} all-to-all(bf16[8,64,128]{2,1,0:T(8,128)(2,1)S(1)} %copy.88), channel_id=1, replica_groups=mesh['eh'=8,'xl'=2,'core'=2,'zh'=8,'zl'=4] {'zh'}, dimensions={0} | all-to-all | bytes 262144 | tf_op jit(solution)/shard_map/all_to_all | solution.py:107
  227.0 0.6 reduce_sum.85
  (24 shorter events, 0.1 us)
Async XLA Ops:
  0.0 2.2 copy-start.4
  2.2 15.3 %copy-start.7 = (s32[64,2]{0,1:T(2,128)S(1)}, s32[64,2]{0,1:T(2,128)}, u32[]{:S(2)}) copy-start(s32[64,2]{0,1:T(2,128)} %param.12) | copy-start | bytes 1540
  2.2 15.9 %copy-start.6 = (bf16[64,128]{1,0:T(8,128)(2,1)S(1)}, bf16[64,128]{1,0:T(8,128)(2,1)}, u32[]{:S(2)}) copy-start(bf16[64,128]{1,0:T(8,128)(2,1)} %param.7) | copy-start | bytes 49156
  2.2 27.9 %copy-start.8 = (s32[64,2]{0,1:T(2,128)S(1)}, s32[64,2]{0,1:T(2,128)}, u32[]{:S(2)}) copy-start(s32[64,2]{0,1:T(2,128)} %param.13) | copy-start | bytes 1540
  2.2 71.5 %copy-start = (bf16[3,56,4096]{2,1,0:T(8,128)(2,1)}, bf16[3,56,4096]{2,1,0:T(8,128)(2,1)S(1)}, u32[]{:S(2)}) copy-start(bf16[3,56,4096]{2,1,0:T(8,128)(2,1)S(1)} %constant_dynamic-update-slice_fusion) | copy-start | bytes 4128772
  2.3 72.2 %copy-start.5 = (f32[4096]{0:T(1024)S(1)}, f32[4096]{0:T(1024)}, u32[]{:S(2)}) copy-start(f32[4096]{0:T(1024)} %param.8) | copy-start | bytes 49156
  2.3 71.2 %collective-permute-start = (bf16[3,56,2048]{2,1,0:T(8,128)(2,1)S(1)}, bf16[3,56,2048]{2,1,0:T(8,128)(2,1)S(1)}, u32[]{:S(2)}, u32[]{:S(2)}) collective-permute-start(bf16[3,56,2048]{2,1,0:T(8,128)(2,1)S(1)} %constant_dynamic-slice_fusion), channel_id=1, source_target_pairs={{0,64},{64,0},{1,65},{65,1},{2,66},{66,2},{3,67},{67,3},{4,68},{68... | collective-permute-start | bytes 2064392 | tf_op jit(solution)/shard_map/ppermute | solution.py:52
  73.6 0.9 copy-start.2
  77.9 8.6 %copy-start.1 = (bf16[3,56,4096]{2,1,0:T(8,128)(2,1)S(1)}, bf16[3,56,4096]{2,1,0:T(8,128)(2,1)}, u32[]{:S(2)}) copy-start(bf16[3,56,4096]{2,1,0:T(8,128)(2,1)} %copy-done) | copy-start | bytes 4128772
  77.9 8.7 %copy-start.3 = (bf16[3,56,2048]{2,1,0:T(8,128)(2,1)S(1)}, bf16[3,56,2048]{2,1,0:T(8,128)(2,1)}, u32[]{:S(2)}) copy-start(bf16[3,56,2048]{2,1,0:T(8,128)(2,1)} %copy-done.2) | copy-start | bytes 2064388
  77.9 30.6 %all-to-all-start = ((bf16[32,24,1024]{2,1,0:T(8,128)(2,1)}), bf16[32,24,1024]{2,1,0:T(8,128)(2,1)}, u32[]{:S(2)}, u32[]{:S(2)}) async-start(bf16[32,24,1024]{2,1,0:T(8,128)(2,1)} %bitcast.1), calls=%async_computation | async-start | bytes 3145728 | tf_op jit(solution)/shard_map/all_to_all | solution.py:79
  87.0 4.0 %collective-permute-start.1 = (bf16[2,3,56,1024]{3,2,0,1:T(8,128)(2,1)S(1)}, bf16[2,3,56,1024]{3,2,0,1:T(8,128)(2,1)S(1)}, u32[]{:S(2)}, u32[]{:S(2)}) collective-permute-start(bf16[2,3,56,1024]{3,2,0,1:T(8,128)(2,1)S(1)} %fusion.7), channel_id=1, source_target_pairs={{0,32},{32,0},{1,33},{33,1},{2,34},{34,2},{3,35},{35,3},{4,36},{36... | collective-permute-start | bytes 2064392 | tf_op jit(solution)/shard_map/ppermute | solution.py:61

commit v2 on v0

v2 whole, which is shorter than its diff:
```python
import jax
import jax.numpy as jnp
from jax import lax
from jax.experimental import pallas as pl
from jax.experimental.pallas import tpu as pltpu
from jax.sharding import Mesh
from jax.sharding import PartitionSpec as P

EXPERTS = 8
TP = ("zh", "zl")
NEAR = 4
LANES = 128
VMEM = pl.BlockSpec(memory_space=pltpu.VMEM)
SMEM = pl.BlockSpec(memory_space=pltpu.SMEM)


def route_ordinal(route_ids):
    flat_ids = route_ids.reshape(-1)
    onehot = (flat_ids[:, None] == jnp.arange(EXPERTS, dtype=jnp.int32)[None, :]).astype(jnp.float32)
    count = flat_ids.shape[0]
    earlier = (jnp.arange(count)[:, None] > jnp.arange(count)[None, :]).astype(jnp.float32)
    before = jnp.dot(earlier, onehot, preferred_element_type=jnp.float32)
    return jnp.sum(before * onehot, axis=1).astype(jnp.int32)


def deal_kernel(place, gain, gate, up, down, own_gain, *outs):
    blocks = gate.shape[1] // (NEAR * LANES)
    for i in range(blocks):
        to = slice(i * LANES, (i + 1) * LANES)
        for r, out in enumerate(outs):
            quarter = lax.rem(place[0] + r, NEAR)
            at = pl.ds(pl.multiple_of((quarter + NEAR * i) * LANES, LANES), LANES)
            for k, weight in enumerate((gate, up, down)):
                out[k, :, to] = weight[:, at]
            if r == 0:
                own_gain[:, to] = gain[:, at]


def gather_kernel(place, gain, *refs):
    pieces, (high, low, down) = refs[:NEAR], refs[NEAR:]
    for r, piece in enumerate(pieces):
        source = lax.rem(place[0] - r + NEAR, NEAR)
        for k in range(2):
            scaled = piece[k].astype(jnp.float32) * gain[...]
            rounded = scaled.astype(jnp.bfloat16)
            high[k, source] = rounded
            low[k, source] = (scaled - rounded.astype(jnp.float32)).astype(jnp.bfloat16)
        down[source] = piece[2]


def act_kernel(rows, high, low, out):
    x = rows[...]
    dims = (((1,), (1,)), ((), ()))
    acts = lax.dot_general(x, high[...], dims, preferred_element_type=jnp.float32)
    acts = acts + lax.dot_general(x, low[...], dims, preferred_element_type=jnp.float32)
    values = x.astype(jnp.float32)
    squares = jnp.sum(values * values, axis=1, keepdims=True)
    rounded = squares.astype(jnp.bfloat16).astype(jnp.float32)
    tail = out.shape[1] - acts.shape[1]
    column = lax.broadcasted_iota(jnp.int32, (x.shape[0], tail), 1)
    extra = jnp.where(column == 0, rounded, jnp.where(column == 1, squares - rounded, 0.0))
    out[:, : acts.shape[1]] = acts.astype(jnp.bfloat16)
    out[:, acts.shape[1] :] = extra.astype(jnp.bfloat16)


def body(attn, norm_gain, w_gate, w_up, w_down, expert_ids, gate_fix):
    owners = lax.axis_size("ep")
    n_zh = lax.axis_size("zh")
    place = lax.axis_index("zl").reshape(1)
    row_tok, cols = attn.shape
    width = norm_gain.shape[0]
    top_count = expert_ids.shape[1]
    cap = 3 * row_tok // 8
    slices = owners // EXPERTS
    part = width // NEAR
    hid = w_gate.shape[1]
    slots = owners * cap
    bf16, f32 = jnp.bfloat16, jnp.float32

    copies = jnp.broadcast_to(attn[None], (n_zh, row_tok, cols))
    rows = lax.all_to_all(copies, "zh", split_axis=0, concat_axis=0, tiled=True)

    piece_type = jax.ShapeDtypeStruct((3, hid, part), bf16)
    own_gain, *pieces = pl.pallas_call(
        deal_kernel,
        in_specs=[SMEM] + [VMEM] * 4,
        out_specs=[VMEM] * (1 + NEAR),
        out_shape=[jax.ShapeDtypeStruct((1, part), f32)] + [piece_type] * NEAR,
        name="deal",
    )(place, norm_gain.reshape(1, width), w_gate[0], w_up[0], w_down[0])
    for r in range(1, NEAR):
        pieces[r] = lax.ppermute(pieces[r], "zl", [(i, (i + r) % NEAR) for i in range(NEAR)])

    ordinal = route_ordinal(expert_ids)
    target = (expert_ids.reshape(-1) * slices) * cap + ordinal
    key = jnp.arange(slots, dtype=jnp.int32)
    key = key - ((key // cap) % slices) * cap
    hits = (target[:, None] == key[None, :]).astype(f32).reshape(row_tok, top_count, slots)
    pick_rows = jnp.sum(hits, axis=1).astype(bf16)
    high = (gate_fix // 256).astype(f32)
    low = (gate_fix % 256).astype(f32)
    combine_map = jnp.concatenate(
        [jnp.sum(hits * high[:, :, None], axis=1), jnp.sum(hits * low[:, :, None], axis=1)], axis=0
    ).astype(bf16)

    rows = rows.transpose(1, 0, 2).reshape(row_tok, part)
    outgoing = lax.dot_general(pick_rows, rows, (((0,), (0,)), ((), ())), preferred_element_type=f32)
    outgoing = outgoing.astype(bf16).reshape(owners, cap, part)
    incoming = lax.all_to_all(outgoing, "ep", split_axis=0, concat_axis=0, tiled=True)

    four = NEAR * hid
    gate_up_high, gate_up_low, down = pl.pallas_call(
        gather_kernel,
        in_specs=[SMEM] + [VMEM] * (1 + NEAR),
        out_specs=[VMEM] * 3,
        out_shape=[jax.ShapeDtypeStruct((2, NEAR, hid, part), bf16)] * 2
        + [jax.ShapeDtypeStruct((NEAR, hid, part), bf16)],
        name="gather",
    )(place, own_gain, *pieces)

    group = slots // NEAR
    lanes = -(-(2 * four + 2) // LANES) * LANES
    acts = pl.pallas_call(
        act_kernel,
        grid=(NEAR,),
        in_specs=[
            pl.BlockSpec((group, part), lambda g: (g, 0)),
            pl.BlockSpec((2 * four, part), lambda g: (0, 0)),
            pl.BlockSpec((2 * four, part), lambda g: (0, 0)),
        ],
        out_specs=pl.BlockSpec((group, lanes), lambda g: (g, 0)),
        out_shape=jax.ShapeDtypeStruct((slots, lanes), bf16),
        name="acts",
    )(incoming.reshape(slots, part), gate_up_high.reshape(2 * four, part), gate_up_low.reshape(2 * four, part))
    acts = lax.all_to_all(acts.reshape(NEAR, group, lanes), "zl", split_axis=0, concat_axis=0, tiled=True)
    sums = jnp.sum(acts.astype(f32), axis=0)
    squares = sums[:, 2 * four : 2 * four + 1] + sums[:, 2 * four + 1 : 2 * four + 2]
    inverse_rms = lax.rsqrt(squares / width + 1e-05)
    gate_act = sums[:, :four] * inverse_rms
    up_act = sums[:, four : 2 * four] * inverse_rms
    hidden_act = (jax.nn.silu(gate_act) * up_act).astype(bf16)
    spread = jnp.broadcast_to(hidden_act[None], (NEAR,) + hidden_act.shape)
    hidden_all = lax.all_to_all(spread, "zl", split_axis=0, concat_axis=0, tiled=True)

    slice_out = jnp.dot(hidden_all.reshape(slots, four), down.reshape(four, part), preferred_element_type=f32)
    slice_out = slice_out.astype(bf16).reshape(owners, cap, part)
    returned = lax.all_to_all(slice_out, "ep", split_axis=0, concat_axis=0, tiled=True)

    both = jnp.dot(combine_map, returned.reshape(slots, part), preferred_element_type=f32)
    combined = both[:row_tok] * (1.0 / 256.0) + both[row_tok:] * (1.0 / 65536.0)
    shares = combined.astype(bf16).reshape(row_tok, n_zh, cols).transpose(1, 0, 2)
    shares = lax.all_to_all(shares, "zh", split_axis=0, concat_axis=0, tiled=True)
    return jnp.sum(shares.astype(f32), axis=0).astype(bf16)


def solution(mesh):
    n_ep, n_tp = mesh.devices.shape
    fine = Mesh(mesh.devices.reshape(n_ep, n_tp // NEAR, NEAR), ("ep", "zh", "zl"))
    in_specs = (
        P("ep", TP),
        P(),
        P("ep", TP, None),
        P("ep", TP, None),
        P("ep", TP, None),
        P("ep", None),
        P("ep", None),
    )
    return jax.shard_map(body, mesh=fine, in_specs=in_specs, out_specs=P("ep", TP), check_vma=False)
```

time: 361 us -> 220 us (0.61)
  the two profiles are of different devices: /device:TPU:1 before, /device:TPU:32 now
where the time goes in v2:
time: 220 us; the launch traced here: 219 us
  blocking collectives  102 us (46%)
  waiting for transfers between devices  52.8 us (24%)
  starting transfers between devices  43.7 us (20%)
  Pallas kernels  11.2 us (5%)
  local copies, waits for them, and re-layouts  4.42 us (2%)
  matrix products  2.85 us (1%)
    all_to_all x1, blocking collectives, body(): lax.all_to_all(shares, 'zh', split_axis=0, concat_axis=0, tiled=True)  35 us
    all_to_all x1, blocking collectives, body(): lax.all_to_all(slice_out, 'ep', split_axis=0, concat_axis=0, tiled=True)  29.7 us
    all_to_all x1, waiting for transfers between devices, body(): rows = lax.all_to_all(copies, 'zh', split_axis=0, concat_axis=0, tiled=True)  27.9 us
    all_to_all x1, starting transfers between devices, body(): rows = lax.all_to_all(copies, 'zh', split_axis=0, concat_axis=0, tiled=True)  27.4 us
    ppermute x3, waiting for transfers between devices, body(): lax.ppermute(pieces[r], 'zl', [(i, (i + r) % NEAR) for i in range(NEAR)])  25 us
    all_to_all x1, blocking collectives, body(): lax.all_to_all(acts.reshape(NEAR, group, lanes), 'zl', split_axis=0, conc...  23.2 us
    all_to_all x1, blocking collectives, body(): lax.all_to_all(spread, 'zl', split_axis=0, concat_axis=0, tiled=True)  13.8 us
    ppermute x3, starting transfers between devices, body(): lax.ppermute(pieces[r], 'zl', [(i, (i + r) % NEAR) for i in range(NEAR)])  8.91 us
  transfers between devices with their start and end apart: 5, of which 4 were waited for; matrix products, arithmetic and copies ran while one was open for 1% of the time, Pallas kernels for 3%

profile of v2, /device:TPU:32, one launch (start us, length us, event | category | flops | bytes accessed | tf_op | source)
XLA Modules:
  0.0 218.8 jit_solution(16679219091554244185)
XLA Ops:
  0.0 1.4 broadcast_in_dim.4
  1.4 27.4 %all-to-all-start = ((bf16[8,64,128]{2,1,0:T(8,128)(2,1)}), bf16[8,64,128]{2,1,0:T(8,128)(2,1)S(1)}, u32[]{:S(2)}, u32[]{:S(2)}) async-start(bf16[8,64,128]{2,1,0:T(8,128)(2,1)} %broadcast_in_dim.4), calls=%async_computation | async-start | bytes 262144 | tf_op jit(solution)/shard_map/all_to_all | solution.py:81
  28.8 0.8 copy.32
  29.6 0.1 eq.33
  29.7 0.1 fusion
  29.9 0.1 convert_element_type.44
  30.0 0.1 copy.33
  30.1 0.7 fusion.26
  30.9 0.2 fusion.1
  31.0 27.9 %all-to-all-done = bf16[8,64,128]{2,1,0:T(8,128)(2,1)S(1)} async-done(((bf16[8,64,128]{2,1,0:T(8,128)(2,1)}), bf16[8,64,128]{2,1,0:T(8,128)(2,1)S(1)}, u32[]{:S(2)}, u32[]{:S(2)}) %all-to-all-start) | async-done | bytes 131104 | tf_op jit(solution)/shard_map/all_to_all | solution.py:81
  58.9 1.7 convolution_convert_fusion
  60.6 7.3 %all-to-all-start.1 = ((bf16[32,24,1024]{2,1,0:T(8,128)(2,1)}), bf16[32,24,1024]{2,1,0:T(8,128)(2,1)S(1)}, u32[]{:S(2)}, u32[]{:S(2)}) async-start(bf16[32,24,1024]{2,1,0:T(8,128)(2,1)} %bitcast.1), calls=%async_computation.1 | async-start | bytes 3145728 | tf_op jit(solution)/shard_map/all_to_all | solution.py:109
  68.0 2.8 %deal.1 = (f32[1,1024]{1,0:T(1,128)}, bf16[3,56,1024]{2,1,0:T(8,128)(2,1)}, bf16[3,56,1024]{2,1,0:T(8,128)(2,1)}, bf16[3,56,1024]{2,1,0:T(8,128)(2,1)}, bf16[3,56,1024]{2,1,0:T(8,128)(2,1)}) custom-call(s32[1]{0:T(128)} %bitcast.3.place, f32[1,4096]{1,0:T(1,128)} %bitcast.44, bf16[56,4096]{1,0:T(8,128)(2,1)} %bitcast.41, bf16[56,4096]{1,0:T(8,128)(2,1)} %bitcast.42, ...), custom_call_target="tpu_custom_call" | custom-call | tf_op jit(solution)/shard_map/deal/pallas_call | solution.py:84
  70.7 2.9 %collective-permute-start = (bf16[3,56,1024]{2,1,0:T(8,128)(2,1)}, bf16[3,56,1024]{2,1,0:T(8,128)(2,1)S(1)}, u32[]{:S(2)}, u32[]{:S(2)}) collective-permute-start(bf16[3,56,1024]{2,1,0:T(8,128)(2,1)} %get-tuple-element.15), channel_id=1, source_target_pairs={{0,1},{1,2},{2,3},{3,0},{4,5},{5,6},{6,7},{7,4},{8,9},{9,10},{10,1... | collective-permute-start | bytes 1032200 | tf_op jit(solution)/shard_map/ppermute | solution.py:92
  73.7 2.0 collective-permute-start.1
  75.7 3.9 %collective-permute-start.2 = (bf16[3,56,1024]{2,1,0:T(8,128)(2,1)}, bf16[3,56,1024]{2,1,0:T(8,128)(2,1)S(1)}, u32[]{:S(2)}, u32[]{:S(2)}) collective-permute-start(bf16[3,56,1024]{2,1,0:T(8,128)(2,1)} %get-tuple-element.17), channel_id=1, source_target_pairs={{0,3},{1,0},{2,1},{3,2},{4,7},{5,4},{6,5},{7,6},{8,11},{9,8},{10,9... | collective-permute-start | bytes 1032200 | tf_op jit(solution)/shard_map/ppermute | solution.py:92
  79.7 4.1 %collective-permute-done.refs_1_ = bf16[3,56,1024]{2,1,0:T(8,128)(2,1)S(1)} collective-permute-done((bf16[3,56,1024]{2,1,0:T(8,128)(2,1)}, bf16[3,56,1024]{2,1,0:T(8,128)(2,1)S(1)}, u32[]{:S(2)}, u32[]{:S(2)}) %collective-permute-start) | collective-permute-done | bytes 344096 | tf_op jit(solution)/shard_map/ppermute | solution.py:92
  83.7 0.0 copy-start.2
  83.7 20.1 %collective-permute-done.1.refs_2_ = bf16[3,56,1024]{2,1,0:T(8,128)(2,1)S(1)} collective-permute-done((bf16[3,56,1024]{2,1,0:T(8,128)(2,1)}, bf16[3,56,1024]{2,1,0:T(8,128)(2,1)S(1)}, u32[]{:S(2)}, u32[]{:S(2)}) %collective-permute-start.1) | collective-permute-done | bytes 344096 | tf_op jit(solution)/shard_map/ppermute | solution.py:92
  103.8 0.0 copy-start.3
  103.8 0.8 collective-permute-done.2.refs_3_
  104.6 0.0 copy-start.4
  104.6 0.0 copy-done.2
  104.6 0.0 copy-done.3
  104.6 0.7 copy-done.4
  105.4 3.0 %gather.1 = (bf16[2,4,56,1024]{3,2,1,0:T(8,128)(2,1)}, bf16[2,4,56,1024]{3,2,1,0:T(8,128)(2,1)}, bf16[4,56,1024]{2,1,0:T(8,128)(2,1)}) custom-call(s32[1]{0:T(128)} %bitcast.3.place, f32[1,1024]{1,0:T(1,128)} %get-tuple-element.13.gain, bf16[3,56,1024]{2,1,0:T(8,128)(2,1)} %get-tuple-element.14.refs_0_, bf16[3,56,1024]{2,1,0:T(8,128)(2,1)} %copy-done.2, ...), custom_call_target="tpu_custom_call" | custom-call | tf_op jit(solution)/shard_map/gather/pallas_call | solution.py:112
  108.4 0.0 all-to-all-done.1
  108.4 0.0 copy-start
  108.4 1.1 copy-done
  109.5 5.4 %acts.1 = bf16[768,512]{1,0:T(8,128)(2,1)} custom-call(bf16[768,1024]{1,0:T(8,128)(2,1)} %bitcast.35, bf16[448,1024]{1,0:T(8,128)(2,1)} %bitcast.38, bf16[448,1024]{1,0:T(8,128)(2,1)} %bitcast.39), custom_call_target="tpu_custom_call" | custom-call | tf_op jit(solution)/shard_map/acts/pallas_call | solution.py:123
  115.0 23.2 %all_to_all.30 = bf16[4,192,512]{2,1,0:T(8,128)(2,1)S(1)} all-to-all(bf16[4,192,512]{2,1,0:T(8,128)(2,1)} %bitcast.36), channel_id=1, replica_groups=mesh['ep'=32,'zh'=8,'zl'=4] {'zl'}, dimensions={0} | all-to-all | bytes 1572864 | tf_op jit(solution)/shard_map/all_to_all | solution.py:135
  138.2 0.0 copy-start.1
  138.2 0.1 convert_reduce_fusion
  138.3 0.2 fusion.18
  138.5 0.2 fusion.7
  138.7 13.8 %all_to_all.31 = bf16[4,192,224]{2,1,0:T(8,128)(2,1)S(1)} all-to-all(bf16[4,192,224]{2,1,0:T(8,128)(2,1)S(1)} %broadcast_in_dim.5), channel_id=1, replica_groups=mesh['ep'=32,'zh'=8,'zl'=4] {'zl'}, dimensions={0} | all-to-all | bytes 688128 | tf_op jit(solution)/shard_map/all_to_all | solution.py:143
  152.5 0.0 copy-done.1
  152.5 0.6 convolution_convert_fusion.1
  153.1 29.7 %all_to_all.32 = bf16[32,24,1024]{2,1,0:T(8,128)(2,1)S(1)} all-to-all(bf16[32,24,1024]{2,1,0:T(8,128)(2,1)S(1)} %bitcast.34), channel_id=1, replica_groups=mesh['ep'=32,'zh'=8,'zl'=4] {'ep'}, dimensions={0} | all-to-all | bytes 3145728 | tf_op jit(solution)/shard_map/all_to_all | solution.py:147
  182.8 0.4 fusion.8
  183.2 35.0 %all_to_all.33 = bf16[8,64,128]{2,1,0:T(8,128)(2,1)S(1)} all-to-all(bf16[8,64,128]{2,1,0:T(8,128)(2,1)S(1)} %bitcast_bitcast_fusion), channel_id=1, replica_groups=mesh['ep'=32,'zh'=8,'zl'=4] {'zh'}, dimensions={0} | all-to-all | bytes 262144 | tf_op jit(solution)/shard_map/all_to_all | solution.py:152
  218.2 0.6 reduce_sum.62
  (4 shorter events, 0.1 us)
Async XLA Ops:
  1.4 57.5 %all-to-all-start = ((bf16[8,64,128]{2,1,0:T(8,128)(2,1)}), bf16[8,64,128]{2,1,0:T(8,128)(2,1)S(1)}, u32[]{:S(2)}, u32[]{:S(2)}) async-start(bf16[8,64,128]{2,1,0:T(8,128)(2,1)} %broadcast_in_dim.4), calls=%async_computation | async-start | bytes 262144 | tf_op jit(solution)/shard_map/all_to_all | solution.py:81
  60.6 47.7 %all-to-all-start.1 = ((bf16[32,24,1024]{2,1,0:T(8,128)(2,1)}), bf16[32,24,1024]{2,1,0:T(8,128)(2,1)S(1)}, u32[]{:S(2)}, u32[]{:S(2)}) async-start(bf16[32,24,1024]{2,1,0:T(8,128)(2,1)} %bitcast.1), calls=%async_computation.1 | async-start | bytes 3145728 | tf_op jit(solution)/shard_map/all_to_all | solution.py:109
  70.7 13.0 %collective-permute-start = (bf16[3,56,1024]{2,1,0:T(8,128)(2,1)}, bf16[3,56,1024]{2,1,0:T(8,128)(2,1)S(1)}, u32[]{:S(2)}, u32[]{:S(2)}) collective-permute-start(bf16[3,56,1024]{2,1,0:T(8,128)(2,1)} %get-tuple-element.15), channel_id=1, source_target_pairs={{0,1},{1,2},{2,3},{3,0},{4,5},{5,6},{6,7},{7,4},{8,9},{9,10},{10,1... | collective-permute-start | bytes 1032200 | tf_op jit(solution)/shard_map/ppermute | solution.py:92
  73.7 30.2 %collective-permute-start.1 = (bf16[3,56,1024]{2,1,0:T(8,128)(2,1)}, bf16[3,56,1024]{2,1,0:T(8,128)(2,1)S(1)}, u32[]{:S(2)}, u32[]{:S(2)}) collective-permute-start(bf16[3,56,1024]{2,1,0:T(8,128)(2,1)} %get-tuple-element.16), channel_id=1, source_target_pairs={{0,2},{1,3},{2,0},{3,1},{4,6},{5,7},{6,4},{7,5},{8,10},{9,11},{10,... | collective-permute-start | bytes 1032200 | tf_op jit(solution)/shard_map/ppermute | solution.py:92
  75.7 28.9 %collective-permute-start.2 = (bf16[3,56,1024]{2,1,0:T(8,128)(2,1)}, bf16[3,56,1024]{2,1,0:T(8,128)(2,1)S(1)}, u32[]{:S(2)}, u32[]{:S(2)}) collective-permute-start(bf16[3,56,1024]{2,1,0:T(8,128)(2,1)} %get-tuple-element.17), channel_id=1, source_target_pairs={{0,3},{1,0},{2,1},{3,2},{4,7},{5,4},{6,5},{7,6},{8,11},{9,8},{10,9... | collective-permute-start | bytes 1032200 | tf_op jit(solution)/shard_map/ppermute | solution.py:92
  83.7 20.9 %copy-start.2 = (bf16[3,56,1024]{2,1,0:T(8,128)(2,1)}, bf16[3,56,1024]{2,1,0:T(8,128)(2,1)S(1)}, u32[]{:S(2)}) copy-start(bf16[3,56,1024]{2,1,0:T(8,128)(2,1)S(1)} %collective-permute-done.refs_1_) | copy-start | bytes 1032196
  103.8 0.8 copy-start.3
  104.6 0.7 copy-start.4
  108.4 1.2 copy-start
  138.2 14.3 %copy-start.1 = (bf16[4,56,1024]{2,1,0:T(8,128)(2,1)S(1)}, bf16[4,56,1024]{2,1,0:T(8,128)(2,1)}, u32[]{:S(2)}) copy-start(bf16[4,56,1024]{2,1,0:T(8,128)(2,1)} %get-tuple-element.20) | copy-start | bytes 1376260

commit v3 on v2

--- a/solution.py
+++ b/solution.py
@@ -7,7 +7,9 @@
 from jax.sharding import PartitionSpec as P
 
 EXPERTS = 8
+EP = ("eh", "xl", "core")
 TP = ("zh", "zl")
+QUAD = ("core", "zl")
 NEAR = 4
 LANES = 128
 VMEM = pl.BlockSpec(memory_space=pltpu.VMEM)
@@ -25,11 +27,13 @@
 
 def deal_kernel(place, gain, gate, up, down, own_gain, *outs):
     blocks = gate.shape[1] // (NEAR * LANES)
-    for i in range(blocks):
-        to = slice(i * LANES, (i + 1) * LANES)
-        for r, out in enumerate(outs):
-            quarter = lax.rem(place[0] + r, NEAR)
-            at = pl.ds(pl.multiple_of((quarter + NEAR * i) * LANES, LANES), LANES)
+    for r, out in enumerate(outs):
+        core = lax.rem(place[0] + r // 2, 2)
+        zl = lax.rem(place[1] + r % 2, 2)
+        for i in range(blocks):
+            to = slice(i * LANES, (i + 1) * LANES)
+            block = (core * blocks + i) * 2 + zl
+            at = pl.ds(pl.multiple_of(block * LANES, LANES), LANES)
             for k, weight in enumerate((gate, up, down)):
                 out[k, :, to] = weight[:, at]
             if r == 0:
@@ -39,7 +43,7 @@
 def gather_kernel(place, gain, *refs):
     pieces, (high, low, down) = refs[:NEAR], refs[NEAR:]
     for r, piece in enumerate(pieces):
-        source = lax.rem(place[0] - r + NEAR, NEAR)
+        source = 2 * lax.rem(place[0] + r // 2, 2) + lax.rem(place[1] + r % 2, 2)
         for k in range(2):
             scaled = piece[k].astype(jnp.float32) * gain[...]
             rounded = scaled.astype(jnp.bfloat16)
@@ -64,9 +68,9 @@
 
 
 def body(attn, norm_gain, w_gate, w_up, w_down, expert_ids, gate_fix):
-    owners = lax.axis_size("ep")
+    owners = lax.axis_size(EP)
     n_zh = lax.axis_size("zh")
-    place = lax.axis_index("zl").reshape(1)
+    place = jnp.stack([lax.axis_index("core"), lax.axis_index("zl")])
     row_tok, cols = attn.shape
     width = norm_gain.shape[0]
     top_count = expert_ids.shape[1]
@@ -89,24 +93,28 @@
         name="deal",
     )(place, norm_gain.reshape(1, width), w_gate[0], w_up[0], w_down[0])
     for r in range(1, NEAR):
-        pieces[r] = lax.ppermute(pieces[r], "zl", [(i, (i + r) % NEAR) for i in range(NEAR)])
+        pieces[r] = lax.ppermute(pieces[r], QUAD, [(i, i ^ r) for i in range(NEAR)])
+    rows, *pieces[1:] = lax.optimization_barrier((rows, *pieces[1:]))
 
     ordinal = route_ordinal(expert_ids)
     target = (expert_ids.reshape(-1) * slices) * cap + ordinal
     key = jnp.arange(slots, dtype=jnp.int32)
     key = key - ((key // cap) % slices) * cap
     hits = (target[:, None] == key[None, :]).astype(f32).reshape(row_tok, top_count, slots)
-    pick_rows = jnp.sum(hits, axis=1).astype(bf16)
+    side = (jnp.arange(2, dtype=jnp.int32)[:, None] == (jnp.arange(slots, dtype=jnp.int32) // cap) % 2).astype(f32)
+    pick_rows = (jnp.sum(hits, axis=1)[None] * side[:, None]).reshape(2 * row_tok, slots).astype(bf16)
     high = (gate_fix // 256).astype(f32)
     low = (gate_fix % 256).astype(f32)
-    combine_map = jnp.concatenate(
-        [jnp.sum(hits * high[:, :, None], axis=1), jnp.sum(hits * low[:, :, None], axis=1)], axis=0
-    ).astype(bf16)
+    weights = jnp.stack(
+        [jnp.sum(hits * high[:, :, None], axis=1), jnp.sum(hits * low[:, :, None], axis=1)]
+    )
+    combine_map = (weights[:, None] * side[None, :, None]).reshape(4 * row_tok, slots).astype(bf16)
 
-    rows = rows.transpose(1, 0, 2).reshape(row_tok, part)
+    half_zh = n_zh // 2
+    rows = rows.reshape(2, half_zh, row_tok, cols).transpose(0, 2, 1, 3).reshape(2 * row_tok, part)
     outgoing = lax.dot_general(pick_rows, rows, (((0,), (0,)), ((), ())), preferred_element_type=f32)
     outgoing = outgoing.astype(bf16).reshape(owners, cap, part)
-    incoming = lax.all_to_all(outgoing, "ep", split_axis=0, concat_axis=0, tiled=True)
+    incoming = lax.all_to_all(outgoing, EP, split_axis=0, concat_axis=0, tiled=True)
 
     four = NEAR * hid
     gate_up_high, gate_up_low, down = pl.pallas_call(
@@ -132,7 +140,7 @@
         out_shape=jax.ShapeDtypeStruct((slots, lanes), bf16),
         name="acts",
     )(incoming.reshape(slots, part), gate_up_high.reshape(2 * four, part), gate_up_low.reshape(2 * four, part))
-    acts = lax.all_to_all(acts.reshape(NEAR, group, lanes), "zl", split_axis=0, concat_axis=0, tiled=True)
+    acts = lax.all_to_all(acts.reshape(NEAR, group, lanes), QUAD, split_axis=0, concat_axis=0, tiled=True)
     sums = jnp.sum(acts.astype(f32), axis=0)
     squares = sums[:, 2 * four : 2 * four + 1] + sums[:, 2 * four + 1 : 2 * four + 2]
     inverse_rms = lax.rsqrt(squares / width + 1e-05)
@@ -140,29 +148,30 @@
     up_act = sums[:, four : 2 * four] * inverse_rms
     hidden_act = (jax.nn.silu(gate_act) * up_act).astype(bf16)
     spread = jnp.broadcast_to(hidden_act[None], (NEAR,) + hidden_act.shape)
-    hidden_all = lax.all_to_all(spread, "zl", split_axis=0, concat_axis=0, tiled=True)
+    hidden_all = lax.all_to_all(spread, QUAD, split_axis=0, concat_axis=0, tiled=True)
 
     slice_out = jnp.dot(hidden_all.reshape(slots, four), down.reshape(four, part), preferred_element_type=f32)
     slice_out = slice_out.astype(bf16).reshape(owners, cap, part)
-    returned = lax.all_to_all(slice_out, "ep", split_axis=0, concat_axis=0, tiled=True)
+    returned = lax.all_to_all(slice_out, EP, split_axis=0, concat_axis=0, tiled=True)
 
     both = jnp.dot(combine_map, returned.reshape(slots, part), preferred_element_type=f32)
-    combined = both[:row_tok] * (1.0 / 256.0) + both[row_tok:] * (1.0 / 65536.0)
-    shares = combined.astype(bf16).reshape(row_tok, n_zh, cols).transpose(1, 0, 2)
+    both = both.reshape(2, 2, row_tok, half_zh, cols)
+    combined = both[0] * (1.0 / 256.0) + both[1] * (1.0 / 65536.0)
+    shares = combined.astype(bf16).transpose(0, 2, 1, 3).reshape(n_zh, row_tok, cols)
     shares = lax.all_to_all(shares, "zh", split_axis=0, concat_axis=0, tiled=True)
     return jnp.sum(shares.astype(f32), axis=0).astype(bf16)
 
 
 def solution(mesh):
     n_ep, n_tp = mesh.devices.shape
-    fine = Mesh(mesh.devices.reshape(n_ep, n_tp // NEAR, NEAR), ("ep", "zh", "zl"))
+    fine = Mesh(mesh.devices.reshape(n_ep // 4, 2, 2, n_tp // 2, 2), EP + TP)
     in_specs = (
-        P("ep", TP),
+        P(EP, TP),
         P(),
-        P("ep", TP, None),
-        P("ep", TP, None),
-        P("ep", TP, None),
-        P("ep", None),
-        P("ep", None),
+        P(EP, TP, None),
+        P(EP, TP, None),
+        P(EP, TP, None),
+        P(EP, None),
+        P(EP, None),
     )
-    return jax.shard_map(body, mesh=fine, in_specs=in_specs, out_specs=P("ep", TP), check_vma=False)
+    return jax.shard_map(body, mesh=fine, in_specs=in_specs, out_specs=P(EP, TP), check_vma=False)

time: 220 us -> 224 us (1.018)
  the two profiles are of different devices: /device:TPU:32 before, /device:TPU:8 now
where the time goes in v3:
time: 224 us; the launch traced here: 223 us
  blocking collectives  86.4 us (39%)
  waiting for transfers between devices  64.8 us (29%)
  starting transfers between devices  50.6 us (23%)
  Pallas kernels  11.3 us (5%)
  matrix products  4.19 us (2%)
  local copies, waits for them, and re-layouts  3.41 us (2%)
    all_to_all x1, blocking collectives, body(): lax.all_to_all(shares, 'zh', split_axis=0, concat_axis=0, tiled=True)  61.2 us
    all_to_all x1, starting transfers between devices, body(): rows = lax.all_to_all(copies, 'zh', split_axis=0, concat_axis=0, tiled=True)  28.4 us
    ppermute x3, waiting for transfers between devices, body(): pieces[r] = lax.ppermute(pieces[r], QUAD, [(i, i ^ r) for i in range(NEAR)])  25.8 us
    all_to_all x1, waiting for transfers between devices, body(): lax.all_to_all(slice_out, EP, split_axis=0, concat_axis=0, tiled=True)  21 us
    all_to_all x1, waiting for transfers between devices, body(): lax.all_to_all(outgoing, EP, split_axis=0, concat_axis=0, tiled=True)  18 us
    all_to_all x1, blocking collectives, body(): lax.all_to_all(acts.reshape(NEAR, group, lanes), QUAD, split_axis=0, conc...  15.4 us
    all_to_all x1, blocking collectives, body(): lax.all_to_all(spread, QUAD, split_axis=0, concat_axis=0, tiled=True)  9.8 us
    ppermute x3, starting transfers between devices, body(): pieces[r] = lax.ppermute(pieces[r], QUAD, [(i, i ^ r) for i in range(NEAR)])  7.85 us
  transfers between devices with their start and end apart: 6, of which 4 were waited for; matrix products, arithmetic and copies ran while one was open for 1% of the time, Pallas kernels for 3%

profile of v3, /device:TPU:8, one launch (start us, length us, event | category | flops | bytes accessed | tf_op | source)
XLA Modules:
  0.0 222.9 jit_solution(17502095499937070108)
XLA Ops:
  0.0 0.0 copy-start.5
  0.0 0.0 copy-start.6
  0.0 1.5 broadcast_in_dim.4
  1.5 28.4 %all-to-all-start = ((bf16[16,64,128]{2,1,0:T(8,128)(2,1)}), bf16[16,64,128]{2,1,0:T(8,128)(2,1)S(1)}, u32[]{:S(2)}, u32[]{:S(2)}) async-start(bf16[16,64,128]{2,1,0:T(8,128)(2,1)} %broadcast_in_dim.4), calls=%async_computation | async-start | bytes 524288 | tf_op jit(solution)/shard_map/all_to_all | solution.py:85
  30.0 0.6 pad_add_fusion.place
  30.5 2.8 %deal.1 = (f32[1,1024]{1,0:T(1,128)}, bf16[3,56,1024]{2,1,0:T(8,128)(2,1)}, bf16[3,56,1024]{2,1,0:T(8,128)(2,1)}, bf16[3,56,1024]{2,1,0:T(8,128)(2,1)}, bf16[3,56,1024]{2,1,0:T(8,128)(2,1)}) custom-call(s32[2]{0:T(128)} %pad_add_fusion.place, f32[1,4096]{1,0:T(1,128)} %bitcast.57, bf16[56,4096]{1,0:T(8,128)(2,1)} %bitcast.54, bf16[56,4096]{1,0:T(8,128)(2,1)} %bitcast.55, ...), custom_call_target="tpu_custom_call" | custom-call | tf_op jit(solution)/shard_map/deal/pallas_call | solution.py:88
  33.3 2.9 %collective-permute-start = (bf16[3,56,1024]{2,1,0:T(8,128)(2,1)}, bf16[3,56,1024]{2,1,0:T(8,128)(2,1)S(1)}, u32[]{:S(2)}, u32[]{:S(2)}) collective-permute-start(bf16[3,56,1024]{2,1,0:T(8,128)(2,1)} %get-tuple-element.17), channel_id=1, source_target_pairs={{0,1},{1,0},{32,33},{33,32},{2,3},{3,2},{34,35},{35,34},{4,5},{5,4... | collective-permute-start | bytes 1032200 | tf_op jit(solution)/shard_map/ppermute | solution.py:96
  36.2 1.9 collective-permute-start.1
  38.2 3.0 %collective-permute-start.2 = (bf16[3,56,1024]{2,1,0:T(8,128)(2,1)}, bf16[3,56,1024]{2,1,0:T(8,128)(2,1)S(1)}, u32[]{:S(2)}, u32[]{:S(2)}) collective-permute-start(bf16[3,56,1024]{2,1,0:T(8,128)(2,1)} %get-tuple-element.19), channel_id=1, source_target_pairs={{0,33},{1,32},{32,1},{33,0},{2,35},{3,34},{34,3},{35,2},{4,37},{5,... | collective-permute-start | bytes 1032200 | tf_op jit(solution)/shard_map/ppermute | solution.py:96
  41.2 0.0 copy-done.5
  41.2 0.1 copy.41
  41.3 0.1 eq.61
  41.4 0.1 fusion
  41.6 0.1 convert_element_type.80
  41.7 0.1 copy.42
  41.9 0.0 copy-done.6
  41.9 0.1 fusion.5
  42.1 20.1 %collective-permute-done.refs_1_ = bf16[3,56,1024]{2,1,0:T(8,128)(2,1)S(1)} collective-permute-done((bf16[3,56,1024]{2,1,0:T(8,128)(2,1)}, bf16[3,56,1024]{2,1,0:T(8,128)(2,1)S(1)}, u32[]{:S(2)}, u32[]{:S(2)}) %collective-permute-start) | collective-permute-done | bytes 344096 | tf_op jit(solution)/shard_map/ppermute | solution.py:96
  62.2 0.0 copy-start.2
  62.2 0.0 collective-permute-done.1.refs_2_
  62.2 0.0 copy-start.3
  62.2 5.7 %collective-permute-done.2.refs_3_ = bf16[3,56,1024]{2,1,0:T(8,128)(2,1)S(1)} collective-permute-done((bf16[3,56,1024]{2,1,0:T(8,128)(2,1)}, bf16[3,56,1024]{2,1,0:T(8,128)(2,1)S(1)}, u32[]{:S(2)}, u32[]{:S(2)}) %collective-permute-start.2) | collective-permute-done | bytes 344096 | tf_op jit(solution)/shard_map/ppermute | solution.py:96
  67.9 0.0 copy-start.4
  67.9 0.0 all-to-all-done
  67.9 0.2 copy.43
  68.1 1.8 convolution_convert_fusion
  69.8 0.0 copy-done.2
  69.8 0.0 copy-done.3
  69.8 0.0 copy-done.4
  69.8 7.8 %all-to-all-start.1 = ((bf16[32,24,1024]{2,1,0:T(8,128)(2,1)}), bf16[32,24,1024]{2,1,0:T(8,128)(2,1)S(1)}, u32[]{:S(2)}, u32[]{:S(2)}) async-start(bf16[32,24,1024]{2,1,0:T(8,128)(2,1)} %bitcast.12), calls=%async_computation.1 | async-start | bytes 3145728 | tf_op jit(solution)/shard_map/all_to_all | solution.py:117
  77.7 3.1 %gather.1 = (bf16[2,4,56,1024]{3,2,1,0:T(8,128)(2,1)}, bf16[2,4,56,1024]{3,2,1,0:T(8,128)(2,1)}, bf16[4,56,1024]{2,1,0:T(8,128)(2,1)}) custom-call(s32[2]{0:T(128)} %pad_add_fusion.place, f32[1,1024]{1,0:T(1,128)} %get-tuple-element.21.gain, bf16[3,56,1024]{2,1,0:T(8,128)(2,1)} %get-tuple-element.22.refs_0_, bf16[3,56,1024]{2,1,0:T(8,128)(2,1)} %copy-done.2, ...), custom_call_target="tpu_custom_call" | custom-call | tf_op jit(solution)/shard_map/gather/pallas_call | solution.py:120
  80.7 18.0 %all-to-all-done.1 = bf16[32,24,1024]{2,1,0:T(8,128)(2,1)S(1)} async-done(((bf16[32,24,1024]{2,1,0:T(8,128)(2,1)}), bf16[32,24,1024]{2,1,0:T(8,128)(2,1)S(1)}, u32[]{:S(2)}, u32[]{:S(2)}) %all-to-all-start.1) | async-done | bytes 1572896 | tf_op jit(solution)/shard_map/all_to_all | solution.py:117
  98.8 0.0 copy-start
  98.8 1.2 copy-done
  99.9 5.5 %acts.1 = bf16[768,512]{1,0:T(8,128)(2,1)} custom-call(bf16[768,1024]{1,0:T(8,128)(2,1)} %bitcast.40, bf16[448,1024]{1,0:T(8,128)(2,1)} %bitcast.48, bf16[448,1024]{1,0:T(8,128)(2,1)} %bitcast.49), custom_call_target="tpu_custom_call" | custom-call | tf_op jit(solution)/shard_map/acts/pallas_call | solution.py:131
  105.4 15.4 %all_to_all.30 = bf16[4,192,512]{2,1,0:T(8,128)(2,1)S(1)} all-to-all(bf16[4,192,512]{2,1,0:T(8,128)(2,1)} %bitcast.41), channel_id=1, replica_groups=mesh['eh'=8,'xl'=2,'core'=2,'zh'=16,'zl'=2] {'core','zl'}, dimensions={0} | all-to-all | bytes 1572864 | tf_op jit(solution)/shard_map/all_to_all | solution.py:143
  120.7 0.1 convert_reduce_fusion
  120.8 0.2 fusion.14
  121.0 0.2 fusion.10
  121.2 9.8 %all_to_all.31 = bf16[4,192,224]{2,1,0:T(8,128)(2,1)S(1)} all-to-all(bf16[4,192,224]{2,1,0:T(8,128)(2,1)S(1)} %broadcast_in_dim.5), channel_id=1, replica_groups=mesh['eh'=8,'xl'=2,'core'=2,'zh'=16,'zl'=2] {'core','zl'}, dimensions={0} | all-to-all | bytes 688128 | tf_op jit(solution)/shard_map/all_to_all | solution.py:151
  131.0 0.0 copy-done.1
  131.0 1.7 convolution_convert_fusion.1
  132.8 6.5 %all-to-all-start.4 = ((bf16[32,24,1024]{2,1,0:T(8,128)(2,1)}), bf16[32,24,1024]{2,1,0:T(8,128)(2,1)S(1)}, u32[]{:S(2)}, u32[]{:S(2)}) async-start(bf16[32,24,1024]{2,1,0:T(8,128)(2,1)} %bitcast.19), calls=%async_computation.4 | async-start | bytes 3145728 | tf_op jit(solution)/shard_map/all_to_all | solution.py:155
  139.3 21.0 %all-to-all-done.4 = bf16[32,24,1024]{2,1,0:T(8,128)(2,1)S(1)} async-done(((bf16[32,24,1024]{2,1,0:T(8,128)(2,1)}), bf16[32,24,1024]{2,1,0:T(8,128)(2,1)S(1)}, u32[]{:S(2)}, u32[]{:S(2)}) %all-to-all-start.4) | async-done | bytes 1572896 | tf_op jit(solution)/shard_map/all_to_all | solution.py:155
  160.3 0.6 fusion.22
  160.9 0.1 fusion.6
  161.1 61.2 %all_to_all.32 = bf16[16,64,128]{2,1,0:T(8,128)(2,1)S(1)} all-to-all(bf16[16,64,128]{2,1,0:T(8,128)(2,1)S(1)} %bitcast.46), channel_id=1, replica_groups=mesh['eh'=8,'xl'=2,'core'=2,'zh'=16,'zl'=2] {'zh'}, dimensions={0} | all-to-all | bytes 524288 | tf_op jit(solution)/shard_map/all_to_all | solution.py:161
  222.3 0.6 reduce_sum.62
  (12 shorter events, 0.3 us)
Async XLA Ops:
  0.0 41.2 %copy-start.5 = (s32[64,2]{0,1:T(2,128)S(1)}, s32[64,2]{0,1:T(2,128)}, u32[]{:S(2)}) copy-start(s32[64,2]{0,1:T(2,128)} %param.12) | copy-start | bytes 1540
  0.0 41.9 %copy-start.6 = (s32[64,2]{0,1:T(2,128)S(1)}, s32[64,2]{0,1:T(2,128)}, u32[]{:S(2)}) copy-start(s32[64,2]{0,1:T(2,128)} %param.13) | copy-start | bytes 1540
  1.5 66.4 %all-to-all-start = ((bf16[16,64,128]{2,1,0:T(8,128)(2,1)}), bf16[16,64,128]{2,1,0:T(8,128)(2,1)S(1)}, u32[]{:S(2)}, u32[]{:S(2)}) async-start(bf16[16,64,128]{2,1,0:T(8,128)(2,1)} %broadcast_in_dim.4), calls=%async_computation | async-start | bytes 524288 | tf_op jit(solution)/shard_map/all_to_all | solution.py:85
  33.3 28.9 %collective-permute-start = (bf16[3,56,1024]{2,1,0:T(8,128)(2,1)}, bf16[3,56,1024]{2,1,0:T(8,128)(2,1)S(1)}, u32[]{:S(2)}, u32[]{:S(2)}) collective-permute-start(bf16[3,56,1024]{2,1,0:T(8,128)(2,1)} %get-tuple-element.17), channel_id=1, source_target_pairs={{0,1},{1,0},{32,33},{33,32},{2,3},{3,2},{34,35},{35,34},{4,5},{5,4... | collective-permute-start | bytes 1032200 | tf_op jit(solution)/shard_map/ppermute | solution.py:96
  36.2 26.0 %collective-permute-start.1 = (bf16[3,56,1024]{2,1,0:T(8,128)(2,1)}, bf16[3,56,1024]{2,1,0:T(8,128)(2,1)S(1)}, u32[]{:S(2)}, u32[]{:S(2)}) collective-permute-start(bf16[3,56,1024]{2,1,0:T(8,128)(2,1)} %get-tuple-element.18), channel_id=1, source_target_pairs={{0,32},{1,33},{32,0},{33,1},{2,34},{3,35},{34,2},{35,3},{4,36},{5,... | collective-permute-start | bytes 1032200 | tf_op jit(solution)/shard_map/ppermute | solution.py:96
  38.2 29.8 %collective-permute-start.2 = (bf16[3,56,1024]{2,1,0:T(8,128)(2,1)}, bf16[3,56,1024]{2,1,0:T(8,128)(2,1)S(1)}, u32[]{:S(2)}, u32[]{:S(2)}) collective-permute-start(bf16[3,56,1024]{2,1,0:T(8,128)(2,1)} %get-tuple-element.19), channel_id=1, source_target_pairs={{0,33},{1,32},{32,1},{33,0},{2,35},{3,34},{34,3},{35,2},{4,37},{5,... | collective-permute-start | bytes 1032200 | tf_op jit(solution)/shard_map/ppermute | solution.py:96
  62.2 7.6 %copy-start.2 = (bf16[3,56,1024]{2,1,0:T(8,128)(2,1)}, bf16[3,56,1024]{2,1,0:T(8,128)(2,1)S(1)}, u32[]{:S(2)}) copy-start(bf16[3,56,1024]{2,1,0:T(8,128)(2,1)S(1)} %collective-permute-done.refs_1_) | copy-start | bytes 1032196
  62.2 7.6 %copy-start.3 = (bf16[3,56,1024]{2,1,0:T(8,128)(2,1)}, bf16[3,56,1024]{2,1,0:T(8,128)(2,1)S(1)}, u32[]{:S(2)}) copy-start(bf16[3,56,1024]{2,1,0:T(8,128)(2,1)S(1)} %collective-permute-done.1.refs_2_) | copy-start | bytes 1032196
  67.9 1.9 copy-start.4
  69.8 28.9 %all-to-all-start.1 = ((bf16[32,24,1024]{2,1,0:T(8,128)(2,1)}), bf16[32,24,1024]{2,1,0:T(8,128)(2,1)S(1)}, u32[]{:S(2)}, u32[]{:S(2)}) async-start(bf16[32,24,1024]{2,1,0:T(8,128)(2,1)} %bitcast.12), calls=%async_computation.1 | async-start | bytes 3145728 | tf_op jit(solution)/shard_map/all_to_all | solution.py:117
  98.8 1.2 copy-start
  120.7 10.3 %copy-start.1 = (bf16[4,56,1024]{2,1,0:T(8,128)(2,1)S(1)}, bf16[4,56,1024]{2,1,0:T(8,128)(2,1)}, u32[]{:S(2)}) copy-start(bf16[4,56,1024]{2,1,0:T(8,128)(2,1)} %get-tuple-element.28) | copy-start | bytes 1376260
  132.8 27.6 %all-to-all-start.4 = ((bf16[32,24,1024]{2,1,0:T(8,128)(2,1)}), bf16[32,24,1024]{2,1,0:T(8,128)(2,1)S(1)}, u32[]{:S(2)}, u32[]{:S(2)}) async-start(bf16[32,24,1024]{2,1,0:T(8,128)(2,1)} %bitcast.19), calls=%async_computation.4 | async-start | bytes 3145728 | tf_op jit(solution)/shard_map/all_to_all | solution.py:155

commit v4 on v3

--- a/solution.py
+++ b/solution.py
@@ -8,9 +8,10 @@
 
 EXPERTS = 8
 EP = ("eh", "xl", "core")
-TP = ("zh", "zl")
+TP = ("zh", "zm", "zl")
 QUAD = ("core", "zl")
 NEAR = 4
+SWAP = [(0, 1), (1, 0)]
 LANES = 128
 VMEM = pl.BlockSpec(memory_space=pltpu.VMEM)
 SMEM = pl.BlockSpec(memory_space=pltpu.SMEM)
@@ -32,7 +33,7 @@
         zl = lax.rem(place[1] + r % 2, 2)
         for i in range(blocks):
             to = slice(i * LANES, (i + 1) * LANES)
-            block = (core * blocks + i) * 2 + zl
+            block = i * NEAR + core * 2 + zl
             at = pl.ds(pl.multiple_of(block * LANES, LANES), LANES)
             for k, weight in enumerate((gate, up, down)):
                 out[k, :, to] = weight[:, at]
@@ -70,6 +71,7 @@
 def body(attn, norm_gain, w_gate, w_up, w_down, expert_ids, gate_fix):
     owners = lax.axis_size(EP)
     n_zh = lax.axis_size("zh")
+    zm = lax.axis_index("zm")
     place = jnp.stack([lax.axis_index("core"), lax.axis_index("zl")])
     row_tok, cols = attn.shape
     width = norm_gain.shape[0]
@@ -94,7 +96,6 @@
     )(place, norm_gain.reshape(1, width), w_gate[0], w_up[0], w_down[0])
     for r in range(1, NEAR):
         pieces[r] = lax.ppermute(pieces[r], QUAD, [(i, i ^ r) for i in range(NEAR)])
-    rows, *pieces[1:] = lax.optimization_barrier((rows, *pieces[1:]))
 
     ordinal = route_ordinal(expert_ids)
     target = (expert_ids.reshape(-1) * slices) * cap + ordinal
@@ -110,8 +111,10 @@
     )
     combine_map = (weights[:, None] * side[None, :, None]).reshape(4 * row_tok, slots).astype(bf16)
 
-    half_zh = n_zh // 2
-    rows = rows.reshape(2, half_zh, row_tok, cols).transpose(0, 2, 1, 3).reshape(2 * row_tok, part)
+    other = lax.ppermute(rows, "zm", SWAP)
+    rows = jnp.stack([jnp.where(zm == 0, rows, other), jnp.where(zm == 0, other, rows)])
+    rows = rows.transpose(0, 2, 1, 3).reshape(2 * row_tok, part)
+    rows, *pieces[1:] = lax.optimization_barrier((rows, *pieces[1:]))
     outgoing = lax.dot_general(pick_rows, rows, (((0,), (0,)), ((), ())), preferred_element_type=f32)
     outgoing = outgoing.astype(bf16).reshape(owners, cap, part)
     incoming = lax.all_to_all(outgoing, EP, split_axis=0, concat_axis=0, tiled=True)
@@ -155,16 +158,19 @@
     returned = lax.all_to_all(slice_out, EP, split_axis=0, concat_axis=0, tiled=True)
 
     both = jnp.dot(combine_map, returned.reshape(slots, part), preferred_element_type=f32)
-    both = both.reshape(2, 2, row_tok, half_zh, cols)
+    both = both.reshape(2, 2, row_tok, part)
     combined = both[0] * (1.0 / 256.0) + both[1] * (1.0 / 65536.0)
-    shares = combined.astype(bf16).transpose(0, 2, 1, 3).reshape(n_zh, row_tok, cols)
+    mine = jnp.where(zm == 0, combined[0], combined[1])
+    yours = jnp.where(zm == 0, combined[1], combined[0]).astype(bf16)
+    shares = mine + lax.ppermute(yours, "zm", SWAP).astype(f32)
+    shares = shares.astype(bf16).reshape(row_tok, n_zh, cols).transpose(1, 0, 2)
     shares = lax.all_to_all(shares, "zh", split_axis=0, concat_axis=0, tiled=True)
     return jnp.sum(shares.astype(f32), axis=0).astype(bf16)
 
 
 def solution(mesh):
     n_ep, n_tp = mesh.devices.shape
-    fine = Mesh(mesh.devices.reshape(n_ep // 4, 2, 2, n_tp // 2, 2), EP + TP)
+    fine = Mesh(mesh.devices.reshape(n_ep // 4, 2, 2, n_tp // 4, 2, 2), EP + TP)
     in_specs = (
         P(EP, TP),
         P(),

time: 224 us -> 215 us (0.960)
  blocking collectives: 86.4 us -> 63.9 us
  starting transfers between devices: 50.6 us -> 57.6 us
  waiting for transfers between devices: 64.8 us -> 71.3 us
    ppermute x3, waiting for transfers between devices: 25.8 us -> 0.01 us  [body(): pieces[r] = lax.ppermute(pieces[r], QUAD, [(i, i ^ r) for i in range(NEAR)])]
    all_to_all x1, blocking collectives: 61.2 us -> 39 us  [body(): lax.all_to_all(shares, 'zh', split_axis=0, concat_axis=0, tiled=True)]
    all_to_all x1, waiting for transfers between devices: 0.01 us -> 18.7 us  [body(): rows = lax.all_to_all(copies, 'zh', split_axis=0, concat_axis=0, tiled=True)]
    ppermute x0 -> x2, waiting for transfers between devices: none -> 13.5 us  [the longest x1 8.67 us: body(): shares = mine + lax.ppermute(yours, 'zm', SWAP).astype(f32)]
    ppermute x0 -> x2, starting transfers between devices: none -> 7.13 us  [the longest x1 4.26 us: body(): other = lax.ppermute(rows, 'zm', SWAP)]
  transfers between devices with their start and end apart: 6 -> 8, of which waited for: 4 -> 5; matrix products, arithmetic and copies ran while one was open for 1% -> 1% of each run, Pallas kernels for 3% -> 3%
where the time goes in v4:
time: 215 us; the launch traced here: 214 us
  waiting for transfers between devices  71.3 us (33%)
  blocking collectives  63.9 us (30%)
  starting transfers between devices  57.6 us (27%)
  Pallas kernels  11.2 us (5%)
  matrix products  4.21 us (2%)
  local copies, waits for them, and re-layouts  3.27 us (2%)
  other arithmetic  2.25 us (1%)
    all_to_all x1, blocking collectives, body(): lax.all_to_all(shares, 'zh', split_axis=0, concat_axis=0, tiled=True)  39 us
    all_to_all x1, starting transfers between devices, body(): rows = lax.all_to_all(copies, 'zh', split_axis=0, concat_axis=0, tiled=True)  28.3 us
    all_to_all x1, waiting for transfers between devices, body(): lax.all_to_all(slice_out, EP, split_axis=0, concat_axis=0, tiled=True)  21 us
    all_to_all x1, waiting for transfers between devices, body(): rows = lax.all_to_all(copies, 'zh', split_axis=0, concat_axis=0, tiled=True)  18.7 us
    all_to_all x1, waiting for transfers between devices, body(): lax.all_to_all(outgoing, EP, split_axis=0, concat_axis=0, tiled=True)  18.1 us
    all_to_all x1, blocking collectives, body(): lax.all_to_all(acts.reshape(NEAR, group, lanes), QUAD, split_axis=0, conc...  15.1 us
    all_to_all x1, blocking collectives, body(): lax.all_to_all(spread, QUAD, split_axis=0, concat_axis=0, tiled=True)  9.8 us
    ppermute x1, waiting for transfers between devices, body(): shares = mine + lax.ppermute(yours, 'zm', SWAP).astype(f32)  8.67 us
  transfers between devices with their start and end apart: 8, of which 5 were waited for; matrix products, arithmetic and copies ran while one was open for 1% of the time, Pallas kernels for 3%

profile of v4, /device:TPU:8, one launch (start us, length us, event | category | flops | bytes accessed | tf_op | source)
XLA Modules:
  0.0 214.0 jit_solution(6211017411485985772)
XLA Ops:
  0.0 1.4 broadcast_in_dim.4
  1.4 28.3 %all-to-all-start = ((bf16[8,64,128]{2,1,0:T(8,128)(2,1)}), bf16[8,64,128]{2,1,0:T(8,128)(2,1)S(1)}, u32[]{:S(2)}, u32[]{:S(2)}) async-start(bf16[8,64,128]{2,1,0:T(8,128)(2,1)} %broadcast_in_dim.4), calls=%async_computation | async-start | bytes 262144 | tf_op jit(solution)/shard_map/all_to_all | solution.py:87
  29.8 0.6 pad_add_fusion.place
  30.4 2.8 %deal.1 = (f32[1,1024]{1,0:T(1,128)}, bf16[3,56,1024]{2,1,0:T(8,128)(2,1)}, bf16[3,56,1024]{2,1,0:T(8,128)(2,1)}, bf16[3,56,1024]{2,1,0:T(8,128)(2,1)}, bf16[3,56,1024]{2,1,0:T(8,128)(2,1)}) custom-call(s32[2]{0:T(128)} %pad_add_fusion.place, f32[1,4096]{1,0:T(1,128)} %bitcast.59, bf16[56,4096]{1,0:T(8,128)(2,1)} %bitcast.56, bf16[56,4096]{1,0:T(8,128)(2,1)} %bitcast.57, ...), custom_call_target="tpu_custom_call" | custom-call | tf_op jit(solution)/shard_map/deal/pallas_call | solution.py:90
  33.2 2.9 %collective-permute-start.1 = (bf16[3,56,1024]{2,1,0:T(8,128)(2,1)}, bf16[3,56,1024]{2,1,0:T(8,128)(2,1)S(1)}, u32[]{:S(2)}, u32[]{:S(2)}) collective-permute-start(bf16[3,56,1024]{2,1,0:T(8,128)(2,1)} %get-tuple-element.17), channel_id=1, source_target_pairs={{0,1},{1,0},{32,33},{33,32},{2,3},{3,2},{34,35},{35,34},{4,5},{5,4... | collective-permute-start | bytes 1032200 | tf_op jit(solution)/shard_map/ppermute | solution.py:98
  36.1 1.9 collective-permute-start.2
  38.0 3.0 %collective-permute-start.3 = (bf16[3,56,1024]{2,1,0:T(8,128)(2,1)}, bf16[3,56,1024]{2,1,0:T(8,128)(2,1)S(1)}, u32[]{:S(2)}, u32[]{:S(2)}) collective-permute-start(bf16[3,56,1024]{2,1,0:T(8,128)(2,1)} %get-tuple-element.19), channel_id=1, source_target_pairs={{0,33},{1,32},{32,1},{33,0},{2,35},{3,34},{34,3},{35,2},{4,37},{5,... | collective-permute-start | bytes 1032200 | tf_op jit(solution)/shard_map/ppermute | solution.py:98
  41.0 0.0 copy-done.5
  41.1 0.1 copy.32
  41.1 0.1 eq.68
  41.3 0.1 fusion
  41.5 0.1 convert_element_type.79
  41.6 0.1 copy.33
  41.7 0.0 copy-done.6
  41.8 0.1 fusion.4
  41.9 18.7 %all-to-all-done = bf16[8,64,128]{2,1,0:T(8,128)(2,1)S(1)} async-done(((bf16[8,64,128]{2,1,0:T(8,128)(2,1)}), bf16[8,64,128]{2,1,0:T(8,128)(2,1)S(1)}, u32[]{:S(2)}, u32[]{:S(2)}) %all-to-all-start) | async-done | bytes 131104 | tf_op jit(solution)/shard_map/all_to_all | solution.py:87
  60.6 4.3 %collective-permute-start = (bf16[8,64,128]{2,1,0:T(8,128)(2,1)S(1)}, bf16[8,64,128]{2,1,0:T(8,128)(2,1)S(1)}, u32[]{:S(2)}, u32[]{:S(2)}) collective-permute-start(bf16[8,64,128]{2,1,0:T(8,128)(2,1)S(1)} %all-to-all-done), channel_id=1, source_target_pairs={{0,2},{2,0},{1,3},{3,1},{4,6},{6,4},{5,7},{7,5},{8,10},{10,8},{9,1... | collective-permute-start | bytes 393224 | tf_op jit(solution)/shard_map/ppermute | solution.py:114
  64.9 4.8 %collective-permute-done = bf16[8,64,128]{2,1,0:T(8,128)(2,1)S(1)} collective-permute-done((bf16[8,64,128]{2,1,0:T(8,128)(2,1)S(1)}, bf16[8,64,128]{2,1,0:T(8,128)(2,1)S(1)}, u32[]{:S(2)}, u32[]{:S(2)}) %collective-permute-start) | collective-permute-done | bytes 131104 | tf_op jit(solution)/shard_map/ppermute | solution.py:114
  69.8 0.2 copy.34
  70.1 0.0 collective-permute-done.1.refs_1_
  70.1 0.0 copy-start.2
  70.1 0.0 collective-permute-done.2.refs_2_
  70.1 0.0 copy-start.3
  70.1 0.0 collective-permute-done.3.refs_3_
  70.1 0.0 copy-start.4
  70.1 1.8 convolution_convert_fusion
  71.9 0.0 copy-done.2
  71.9 0.0 copy-done.3
  71.9 0.0 copy-done.4
  71.9 7.5 %all-to-all-start.1 = ((bf16[32,24,1024]{2,1,0:T(8,128)(2,1)}), bf16[32,24,1024]{2,1,0:T(8,128)(2,1)S(1)}, u32[]{:S(2)}, u32[]{:S(2)}) async-start(bf16[32,24,1024]{2,1,0:T(8,128)(2,1)} %bitcast.13), calls=%async_computation.1 | async-start | bytes 3145728 | tf_op jit(solution)/shard_map/all_to_all | solution.py:120
  79.4 3.0 %gather.1 = (bf16[2,4,56,1024]{3,2,1,0:T(8,128)(2,1)}, bf16[2,4,56,1024]{3,2,1,0:T(8,128)(2,1)}, bf16[4,56,1024]{2,1,0:T(8,128)(2,1)}) custom-call(s32[2]{0:T(128)} %pad_add_fusion.place, f32[1,1024]{1,0:T(1,128)} %get-tuple-element.21.gain, bf16[3,56,1024]{2,1,0:T(8,128)(2,1)} %get-tuple-element.22.refs_0_, bf16[3,56,1024]{2,1,0:T(8,128)(2,1)} %copy-done.2, ...), custom_call_target="tpu_custom_call" | custom-call | tf_op jit(solution)/shard_map/gather/pallas_call | solution.py:123
  82.4 18.1 %all-to-all-done.1 = bf16[32,24,1024]{2,1,0:T(8,128)(2,1)S(1)} async-done(((bf16[32,24,1024]{2,1,0:T(8,128)(2,1)}), bf16[32,24,1024]{2,1,0:T(8,128)(2,1)S(1)}, u32[]{:S(2)}, u32[]{:S(2)}) %all-to-all-start.1) | async-done | bytes 1572896 | tf_op jit(solution)/shard_map/all_to_all | solution.py:120
  100.5 1.1 copy-done
  101.7 5.5 %acts.1 = bf16[768,512]{1,0:T(8,128)(2,1)} custom-call(bf16[768,1024]{1,0:T(8,128)(2,1)} %bitcast.44, bf16[448,1024]{1,0:T(8,128)(2,1)} %bitcast.50, bf16[448,1024]{1,0:T(8,128)(2,1)} %bitcast.51), custom_call_target="tpu_custom_call" | custom-call | tf_op jit(solution)/shard_map/acts/pallas_call | solution.py:134
  107.1 15.1 %all_to_all.30 = bf16[4,192,512]{2,1,0:T(8,128)(2,1)S(1)} all-to-all(bf16[4,192,512]{2,1,0:T(8,128)(2,1)} %bitcast.45), channel_id=1, replica_groups=mesh['eh'=8,'xl'=2,'core'=2,'zh'=8,'zm'=2,'zl'=2] {'core','zl'}, dimensions={0} | all-to-all | bytes 1572864 | tf_op jit(solution)/shard_map/all_to_all | solution.py:146
  122.2 0.1 convert_reduce_fusion
  122.3 0.2 fusion.11
  122.5 0.2 fusion.6
  122.7 9.8 %all_to_all.31 = bf16[4,192,224]{2,1,0:T(8,128)(2,1)S(1)} all-to-all(bf16[4,192,224]{2,1,0:T(8,128)(2,1)S(1)} %broadcast_in_dim.5), channel_id=1, replica_groups=mesh['eh'=8,'xl'=2,'core'=2,'zh'=8,'zm'=2,'zl'=2] {'core','zl'}, dimensions={0} | all-to-all | bytes 688128 | tf_op jit(solution)/shard_map/all_to_all | solution.py:154
  132.5 1.7 convolution_convert_fusion.1
  134.3 6.7 %all-to-all-start.4 = ((bf16[32,24,1024]{2,1,0:T(8,128)(2,1)}), bf16[32,24,1024]{2,1,0:T(8,128)(2,1)S(1)}, u32[]{:S(2)}, u32[]{:S(2)}) async-start(bf16[32,24,1024]{2,1,0:T(8,128)(2,1)} %bitcast.20), calls=%async_computation.4 | async-start | bytes 3145728 | tf_op jit(solution)/shard_map/all_to_all | solution.py:158
  141.1 21.0 %all-to-all-done.4 = bf16[32,24,1024]{2,1,0:T(8,128)(2,1)S(1)} async-done(((bf16[32,24,1024]{2,1,0:T(8,128)(2,1)}), bf16[32,24,1024]{2,1,0:T(8,128)(2,1)S(1)}, u32[]{:S(2)}, u32[]{:S(2)}) %all-to-all-start.4) | async-done | bytes 1572896 | tf_op jit(solution)/shard_map/all_to_all | solution.py:158
  162.1 0.6 fusion.19
  162.7 0.1 fusion.1
  162.8 2.9 %collective-permute-start.4 = (bf16[64,1024]{1,0:T(8,128)(2,1)S(1)}, bf16[64,1024]{1,0:T(8,128)(2,1)S(1)}, u32[]{:S(2)}, u32[]{:S(2)}) collective-permute-start(bf16[64,1024]{1,0:T(8,128)(2,1)S(1)} %select_convert_fusion), channel_id=1, source_target_pairs={{0,2},{2,0},{1,3},{3,1},{4,6},{6,4},{5,7},{7,5},{8,10},{10,8},{9,1... | collective-permute-start | bytes 393224 | tf_op jit(solution)/shard_map/ppermute | solution.py:165
  165.7 8.7 %collective-permute-done.4 = bf16[64,1024]{1,0:T(8,128)(2,1)S(1)} collective-permute-done((bf16[64,1024]{1,0:T(8,128)(2,1)S(1)}, bf16[64,1024]{1,0:T(8,128)(2,1)S(1)}, u32[]{:S(2)}, u32[]{:S(2)}) %collective-permute-start.4) | collective-permute-done | bytes 131104 | tf_op jit(solution)/shard_map/ppermute | solution.py:165
  174.4 39.0 %all_to_all.32 = bf16[8,64,128]{2,1,0:T(8,128)(2,1)S(1)} all-to-all(bf16[8,64,128]{2,1,0:T(8,128)(2,1)S(1)} %bitcast_bitcast_fusion), channel_id=1, replica_groups=mesh['eh'=8,'xl'=2,'core'=2,'zh'=8,'zm'=2,'zl'=2] {'zh'}, dimensions={0} | all-to-all | bytes 262144 | tf_op jit(solution)/shard_map/all_to_all | solution.py:167
  213.4 0.6 reduce_sum.62
  (19 shorter events, 0.4 us)
Async XLA Ops:
  0.0 41.0 %copy-start.5 = (s32[64,2]{0,1:T(2,128)S(1)}, s32[64,2]{0,1:T(2,128)}, u32[]{:S(2)}) copy-start(s32[64,2]{0,1:T(2,128)} %param.12) | copy-start | bytes 1540
  0.0 41.7 %copy-start.6 = (s32[64,2]{0,1:T(2,128)S(1)}, s32[64,2]{0,1:T(2,128)}, u32[]{:S(2)}) copy-start(s32[64,2]{0,1:T(2,128)} %param.13) | copy-start | bytes 1540
  1.4 59.2 %all-to-all-start = ((bf16[8,64,128]{2,1,0:T(8,128)(2,1)}), bf16[8,64,128]{2,1,0:T(8,128)(2,1)S(1)}, u32[]{:S(2)}, u32[]{:S(2)}) async-start(bf16[8,64,128]{2,1,0:T(8,128)(2,1)} %broadcast_in_dim.4), calls=%async_computation | async-start | bytes 262144 | tf_op jit(solution)/shard_map/all_to_all | solution.py:87
  33.2 36.9 %collective-permute-start.1 = (bf16[3,56,1024]{2,1,0:T(8,128)(2,1)}, bf16[3,56,1024]{2,1,0:T(8,128)(2,1)S(1)}, u32[]{:S(2)}, u32[]{:S(2)}) collective-permute-start(bf16[3,56,1024]{2,1,0:T(8,128)(2,1)} %get-tuple-element.17), channel_id=1, source_target_pairs={{0,1},{1,0},{32,33},{33,32},{2,3},{3,2},{34,35},{35,34},{4,5},{5,4... | collective-permute-start | bytes 1032200 | tf_op jit(solution)/shard_map/ppermute | solution.py:98
  36.1 34.0 %collective-permute-start.2 = (bf16[3,56,1024]{2,1,0:T(8,128)(2,1)}, bf16[3,56,1024]{2,1,0:T(8,128)(2,1)S(1)}, u32[]{:S(2)}, u32[]{:S(2)}) collective-permute-start(bf16[3,56,1024]{2,1,0:T(8,128)(2,1)} %get-tuple-element.18), channel_id=1, source_target_pairs={{0,32},{1,33},{32,0},{33,1},{2,34},{3,35},{34,2},{35,3},{4,36},{5,... | collective-permute-start | bytes 1032200 | tf_op jit(solution)/shard_map/ppermute | solution.py:98
  38.0 32.1 %collective-permute-start.3 = (bf16[3,56,1024]{2,1,0:T(8,128)(2,1)}, bf16[3,56,1024]{2,1,0:T(8,128)(2,1)S(1)}, u32[]{:S(2)}, u32[]{:S(2)}) collective-permute-start(bf16[3,56,1024]{2,1,0:T(8,128)(2,1)} %get-tuple-element.19), channel_id=1, source_target_pairs={{0,33},{1,32},{32,1},{33,0},{2,35},{3,34},{34,3},{35,2},{4,37},{5,... | collective-permute-start | bytes 1032200 | tf_op jit(solution)/shard_map/ppermute | solution.py:98
  60.6 9.2 %collective-permute-start = (bf16[8,64,128]{2,1,0:T(8,128)(2,1)S(1)}, bf16[8,64,128]{2,1,0:T(8,128)(2,1)S(1)}, u32[]{:S(2)}, u32[]{:S(2)}) collective-permute-start(bf16[8,64,128]{2,1,0:T(8,128)(2,1)S(1)} %all-to-all-done), channel_id=1, source_target_pairs={{0,2},{2,0},{1,3},{3,1},{4,6},{6,4},{5,7},{7,5},{8,10},{10,8},{9,1... | collective-permute-start | bytes 393224 | tf_op jit(solution)/shard_map/ppermute | solution.py:114
  70.1 1.8 copy-start.2
  70.1 1.8 copy-start.3
  70.1 1.8 copy-start.4
  71.9 28.6 %all-to-all-start.1 = ((bf16[32,24,1024]{2,1,0:T(8,128)(2,1)}), bf16[32,24,1024]{2,1,0:T(8,128)(2,1)S(1)}, u32[]{:S(2)}, u32[]{:S(2)}) async-start(bf16[32,24,1024]{2,1,0:T(8,128)(2,1)} %bitcast.13), calls=%async_computation.1 | async-start | bytes 3145728 | tf_op jit(solution)/shard_map/all_to_all | solution.py:120
  100.5 1.1 copy-start
  122.2 10.3 %copy-start.1 = (bf16[4,56,1024]{2,1,0:T(8,128)(2,1)S(1)}, bf16[4,56,1024]{2,1,0:T(8,128)(2,1)}, u32[]{:S(2)}) copy-start(bf16[4,56,1024]{2,1,0:T(8,128)(2,1)} %get-tuple-element.28) | copy-start | bytes 1376260
  134.3 27.8 %all-to-all-start.4 = ((bf16[32,24,1024]{2,1,0:T(8,128)(2,1)}), bf16[32,24,1024]{2,1,0:T(8,128)(2,1)S(1)}, u32[]{:S(2)}, u32[]{:S(2)}) async-start(bf16[32,24,1024]{2,1,0:T(8,128)(2,1)} %bitcast.20), calls=%async_computation.4 | async-start | bytes 3145728 | tf_op jit(solution)/shard_map/all_to_all | solution.py:158
  162.8 11.5 %collective-permute-start.4 = (bf16[64,1024]{1,0:T(8,128)(2,1)S(1)}, bf16[64,1024]{1,0:T(8,128)(2,1)S(1)}, u32[]{:S(2)}, u32[]{:S(2)}) collective-permute-start(bf16[64,1024]{1,0:T(8,128)(2,1)S(1)} %select_convert_fusion), channel_id=1, source_target_pairs={{0,2},{2,0},{1,3},{3,1},{4,6},{6,4},{5,7},{7,5},{8,10},{10,8},{9,1... | collective-permute-start | bytes 393224 | tf_op jit(solution)/shard_map/ppermute | solution.py:165
